TPU v7x, 128 devices: a whole 4x4x4 slice. The times are simulated.
128 devices in a mesh: dp: 16 (over y, x), inner: 8 (over z, core).
Axes of the slice: x: 4, y: 4, z: 4, core: 2. Of those that a mesh axis runs over, the one named last changes fastest.
Arguments:
- queries: bfloat16 [64, 512, 1024], P('dp', 'inner'), may hold values from -6 to 6
- passages: bfloat16 [64, 512, 1024], P('dp', 'inner'), may hold values from -6 to 6
- neg_lists: int32 [64, 8], replicated, may hold values from 0 to 63, as said below
Outputs:
- mean_loss: float32 [], replicated
- query_grad: bfloat16 [64, 512, 1024], P('dp', 'inner')
- passage_grad: bfloat16 [64, 512, 1024], P('dp', 'inner')
Inputs may be any that keep to these rules, and one draw needn't show every extreme that they name: `neg_lists`: each row lists 8 different passage blocks, none from the row's own group (blocks with the same id // 4). The blocks that the rows of one group list include at least one and at most 2 blocks of every other group; in every draw some group lists exactly 2 blocks of every other group.
All inputs are finite; a program needn't handle non-finite values.
Results may differ from a plain program's by a relative error of at most 0.009.
Values may be sent and summed in bfloat16 or wider, within the bound.
A program may use at most 128 MiB of HBM per device.

v0:
```python
import math

import jax
import jax.numpy as jnp
from jax import lax
from jax.sharding import PartitionSpec as P

CAP = 2


NEG_FILL = -1e30


def slot_tables(neg_lists, groups, per_group, slot_depth):
    block_count = neg_lists.shape[0]
    block_ids = jnp.arange(block_count, dtype=jnp.int32)
    named = jnp.any(neg_lists[:, :, None] == block_ids[None, None, :], axis=1)
    present = jnp.any(named.reshape(groups, per_group, block_count), axis=1)
    present = present.reshape(groups, groups, per_group).astype(jnp.int32)
    slot_ranks = jnp.cumsum(present, axis=2) - 1
    slot_ids = jnp.arange(slot_depth, dtype=jnp.int32)
    hits = (present[..., None] == 1) & (slot_ranks[..., None] == slot_ids[None, None, None, :])
    local_ids = jnp.arange(per_group, dtype=jnp.int32)
    slot_block = jnp.sum(jnp.where(hits, local_ids[None, None, :, None], 0), axis=2)
    slot_live = jnp.any(hits, axis=2)
    return (slot_ranks, slot_block, slot_live)


def body(queries, passages, neg_lists):
    per_group, slice_rows, embed_width = queries.shape
    pick_count = neg_lists.shape[1]
    groups = lax.axis_size("dp")
    inner_count = lax.axis_size("inner")
    full_rows = slice_rows * inner_count
    cand_rows = (pick_count + 1) * slice_rows
    slot_count = groups * CAP
    score_scale = 1.0 / math.sqrt(embed_width)
    my_group = lax.axis_index("dp")
    inner_pos = lax.axis_index("inner")
    slot_ranks, slot_block, slot_live = slot_tables(neg_lists, groups, per_group, CAP)
    listed = lax.dynamic_slice_in_dim(neg_lists, my_group * per_group, per_group, 0)
    owner_group = listed // per_group
    owner_local = listed % per_group
    my_ranks = lax.dynamic_index_in_dim(slot_ranks, my_group, 0, keepdims=False)
    slot_of = owner_group * CAP + my_ranks[owner_group, owner_local]
    sends_for = lax.dynamic_index_in_dim(slot_block, my_group, 1, keepdims=False)
    live_for = lax.dynamic_index_in_dim(slot_live, my_group, 1, keepdims=False)
    block_ids = jnp.arange(per_group, dtype=jnp.int32)
    held_start = jnp.zeros((per_group, pick_count, slice_rows, embed_width), jnp.bfloat16)
    shard_rows = lax.all_gather(passages, "dp", axis=0, tiled=True)
    inside = (listed >= 0) & (listed < shard_rows.shape[0])
    picked = shard_rows[jnp.clip(listed, 0, shard_rows.shape[0] - 1)]
    negatives = jnp.where(inside[:, :, None, None], picked, held_start)
    whole_queries = lax.all_gather(queries, "inner", axis=1, tiled=True)

    def candidates(block_index):
        own_rows = lax.dynamic_index_in_dim(passages, block_index, 0, keepdims=True)
        other_rows = lax.dynamic_index_in_dim(negatives, block_index, 0, keepdims=False)
        return jnp.concatenate([own_rows, other_rows], axis=0).reshape(cand_rows, embed_width)

    def scores(block_index, query_block):
        return (
            jnp.einsum(
                "cd,rd->cr",
                candidates(block_index),
                query_block,
                preferred_element_type=jnp.float32,
            )
            * score_scale
        )

    def forward(inputs):
        block_index, query_block = inputs
        logits = scores(block_index, query_block)
        row_peak = jnp.max(logits, axis=0)
        row_mass = jnp.sum(jnp.exp(logits - row_peak[None, :]), axis=0)
        col_peak = jnp.max(logits, axis=1)
        col_mass = jnp.sum(jnp.exp(logits - col_peak[:, None]), axis=1)
        return (row_peak, row_mass, col_peak, col_mass)

    row_peak, row_mass, col_peak, col_mass = lax.map(forward, (block_ids, whole_queries))
    peak_all = lax.pmax(row_peak, "inner")
    mass_all = lax.psum(row_mass * jnp.exp(row_peak - peak_all), "inner")
    query_lse = peak_all + jnp.log(mass_all)
    own_peak = col_peak[:, :slice_rows]
    own_mass = col_mass[:, :slice_rows]
    far_peak = col_peak[:, slice_rows:].reshape(per_group * pick_count, slice_rows)
    far_mass = col_mass[:, slice_rows:].reshape(per_group * pick_count, slice_rows)
    flat_slots = slot_of.reshape(-1)
    onehot = flat_slots[:, None] == jnp.arange(slot_count, dtype=jnp.int32)[None, :]
    slot_peak = jnp.max(jnp.where(onehot[:, :, None], far_peak[:, None, :], NEG_FILL), axis=0)
    rescaled = far_mass * jnp.exp(far_peak - slot_peak[flat_slots])
    slot_mass = jnp.dot(onehot.astype(jnp.float32).T, rescaled, precision=lax.Precision.HIGHEST)
    got_peak, got_mass = (
        lax.all_to_all(
            slot_peak.reshape(groups, CAP, slice_rows),
            "dp",
            split_axis=0,
            concat_axis=0,
            tiled=True,
        ),
        lax.all_to_all(
            slot_mass.reshape(groups, CAP, slice_rows),
            "dp",
            split_axis=0,
            concat_axis=0,
            tiled=True,
        ),
    )
    belongs = (sends_for[:, :, None] == block_ids[None, None, :]) & live_for[:, :, None]
    belongs = belongs.reshape(slot_count, per_group)
    got_peak = got_peak.reshape(slot_count, slice_rows)
    got_mass = got_mass.reshape(slot_count, slice_rows)
    spread_peak = jnp.where(belongs[:, :, None], got_peak[:, None, :], NEG_FILL)
    pass_peak = jnp.maximum(own_peak, jnp.max(spread_peak, axis=0))
    spread_mass = jnp.where(
        belongs[:, :, None],
        got_mass[:, None, :] * jnp.exp(spread_peak - pass_peak[None, :, :]),
        0.0,
    )
    pass_mass = own_mass * jnp.exp(own_peak - pass_peak) + jnp.sum(spread_mass, axis=0)
    passage_lse = pass_peak + jnp.log(pass_mass)
    own_scores = (
        jnp.einsum("lrd,lrd->lr", queries, passages, preferred_element_type=jnp.float32)
        * score_scale
    )
    my_query_lse = lax.dynamic_slice_in_dim(query_lse, inner_pos * slice_rows, slice_rows, 1)
    local_loss = jnp.sum(my_query_lse - own_scores) + jnp.sum(passage_lse - own_scores)
    mean_loss = lax.psum(local_loss, ("dp", "inner")) / (2.0 * groups * per_group * full_rows)
    lse_out = passage_lse[sends_for]
    lse_back = lax.all_to_all(lse_out, "dp", split_axis=0, concat_axis=0, tiled=True).reshape(
        slot_count, slice_rows
    )
    cand_lse = jnp.concatenate([passage_lse[:, None, :], lse_back[slot_of]], axis=1).reshape(
        per_group, cand_rows
    )
    cand_pos = jnp.arange(cand_rows, dtype=jnp.int32)
    row_pos = jnp.arange(full_rows, dtype=jnp.int32)
    target = (
        (cand_pos[:, None] < slice_rows)
        & (row_pos[None, :] == inner_pos * slice_rows + cand_pos[:, None])
    ).astype(jnp.float32)

    def backward(block_index, carry):
        weights, slot_grad, own_grad = carry
        query_block = lax.dynamic_index_in_dim(whole_queries, block_index, 0, keepdims=False)
        logits = scores(block_index, query_block)
        row_lse = lax.dynamic_index_in_dim(query_lse, block_index, 0, keepdims=False)
        col_lse = lax.dynamic_index_in_dim(cand_lse, block_index, 0, keepdims=False)
        probs = (
            0.5 * jnp.exp(logits - row_lse[None, :])
            + 0.5 * jnp.exp(logits - col_lse[:, None])
            - target
        )
        rounded = probs.astype(jnp.bfloat16)
        passage_part = jnp.einsum(
            "cr,rd->cd", rounded, query_block, preferred_element_type=jnp.float32
        )
        own_grad = lax.dynamic_update_index_in_dim(
            own_grad, passage_part[:slice_rows], block_index, 0
        )
        slot_targets = lax.dynamic_index_in_dim(slot_of, block_index, 0, keepdims=False)
        slot_grad = slot_grad.at[slot_targets].add(
            passage_part[slice_rows:].reshape(pick_count, slice_rows, embed_width)
        )
        weights = lax.dynamic_update_index_in_dim(weights, rounded, block_index, 0)
        return (weights, slot_grad, own_grad)

    start_carry = (
        jnp.zeros((per_group, cand_rows, full_rows), jnp.bfloat16),
        jnp.zeros((slot_count, slice_rows, embed_width), jnp.float32),
        jnp.zeros((per_group, slice_rows, embed_width), jnp.float32),
    )
    weights, slot_grad, own_grad = lax.fori_loop(0, per_group, backward, start_carry)

    def one_block(inputs):
        block_index, block_weights = inputs
        return jnp.einsum(
            "cr,cd->rd", block_weights, candidates(block_index), preferred_element_type=jnp.float32
        )

    query_sum = lax.psum_scatter(
        jnp.swapaxes(lax.map(one_block, (block_ids, weights)), 0, 1).astype(jnp.bfloat16),
        "inner",
        scatter_dimension=0,
        tiled=True,
    ).astype(jnp.float32)
    query_grad = jnp.swapaxes(query_sum, 0, 1).astype(jnp.bfloat16)
    returned = lax.all_to_all(
        slot_grad.astype(jnp.bfloat16).reshape(groups, CAP, slice_rows, embed_width),
        "dp",
        split_axis=0,
        concat_axis=0,
        tiled=True,
    )
    passage_sum = jnp.einsum(
        "eg,ecd->gcd",
        belongs.astype(jnp.bfloat16),
        returned.reshape(slot_count, slice_rows, embed_width),
        preferred_element_type=jnp.float32,
    )
    passage_grad = (passage_sum + own_grad).astype(jnp.bfloat16)
    return (mean_loss, query_grad, passage_grad)


def solution(mesh):
    in_specs = (P("dp", "inner", None), P("dp", "inner", None), P())
    out_specs = (P(), P("dp", "inner", None), P("dp", "inner", None))
    return jax.shard_map(body, mesh=mesh, in_specs=in_specs, out_specs=out_specs, check_vma=False)
```

profile of v0, /device:TPU:0, one launch (start us, length us, event | category | flops | bytes accessed | tf_op | source)
XLA Modules:
  0.0 453.5 jit_solution(6817125540954745259)
XLA Ops:
  13.2 70.1 %all-gather.3.cloned.1.call-done = bf16[64,64,1024]{2,1,0:T(8,128)(2,1)} async-done(((bf16[4,64,1024]{2,1,0:T(8,128)(2,1)}), bf16[64,64,1024]{2,1,0:T(8,128)(2,1)}) %all-gather.3.cloned.1.call-update) | async-done | bytes 8388624 | tf_op jit(solution)/shard_map/all_gather | solution.py:50
  83.4 6.1 %gather_fusion = bf16[32,64,1024]{2,1,0:T(8,128)(2,1)} fusion(bf16[64,64,1024]{2,1,0:T(8,128)(2,1)} %all-gather.3.cloned.1.call-done, s32[1024]{0:T(1024)S(1)} %pad_clamp_fusion.3), kind=kCustom, calls=%fused_computation | custom fusion | bytes 8388736 | tf_op jit(solution)/shard_map/gather | solution.py:52
  94.0 23.1 %all-gather.5.cloned.1.call-done = bf16[4,512,1024]{2,1,0:T(8,128)(2,1)} async-done(((bf16[4,64,1024]{2,1,0:T(8,128)(2,1)}), bf16[4,512,1024]{2,1,0:T(8,128)(2,1)}) %all-gather.5.cloned.1.call-update) | async-done | bytes 4194320 | tf_op jit(solution)/shard_map/all_gather | solution.py:54
  117.1 27.3 %while.44 = (s32[]{:T(128)}, f32[4,512]{1,0:T(4,128)S(1)}, f32[4,512]{1,0:T(4,128)S(1)}, f32[4,576]{1,0:T(4,128)S(1)}, f32[4,576]{1,0:T(4,128)S(1)}, /*index=5*/...) while((s32[]{:T(128)}, f32[4,512]{1,0:T(4,128)S(1)}, ...), condition=%wide.region_5.6_spmd, body=%wide.region_0.5_spmd.sunk | while | flops 606631808 | bytes 9346491 | solution.py:81
  146.5 6.8 %all-to-all-start.1 = ((f32[16,1,128]{2,1,0:T(1,128)}), f32[16,1,128]{2,1,0:T(1,128)S(1)}, u32[]{:S(2)}, u32[]{:S(2)}) async-start(f32[16,1,128]{2,1,0:T(1,128)} %reshape.334), calls=%async_computation.1 | async-start | bytes 16384 | tf_op jit(solution)/shard_map/all_to_all | solution.py:102
  154.0 13.3 %pmax.7 = f32[4,512]{1,0:T(4,128)S(1)} all-reduce(f32[4,512]{1,0:T(4,128)S(1)} %get-tuple-element.271), channel_id=1, replica_groups=mesh['dp'=16,'inner'=8] {'inner'}, use_global_device_ids=true, to_apply=%region_6.7 | all-reduce | flops 2048 | bytes 16384 | tf_op jit(solution)/shard_map/pmax | solution.py:82
  167.3 12.7 %psum.14 = f32[4,512]{1,0:T(4,128)S(1)} all-reduce(f32[4,512]{1,0:T(4,128)S(1)} %exponential_multiply_fusion.1), channel_id=1, replica_groups=mesh['dp'=16,'inner'=8] {'inner'}, use_global_device_ids=true, to_apply=%region_7.8 | all-reduce | flops 2048 | bytes 16384 | tf_op jit(solution)/shard_map/psum | solution.py:83
  180.0 6.7 %all-to-all-start = ((f32[16,1,128]{2,1,0:T(1,128)}), f32[16,1,128]{2,1,0:T(1,128)S(1)}, u32[]{:S(2)}, u32[]{:S(2)}) async-start(f32[16,1,128]{2,1,0:T(1,128)} %reshape.332), calls=%async_computation | async-start | bytes 16384 | tf_op jit(solution)/shard_map/all_to_all | solution.py:95
  187.9 6.2 %all-to-all-done = f32[16,1,128]{2,1,0:T(1,128)S(1)} async-done(((f32[16,1,128]{2,1,0:T(1,128)}), f32[16,1,128]{2,1,0:T(1,128)S(1)}, u32[]{:S(2)}, u32[]{:S(2)}) %all-to-all-start) | async-done | bytes 8224 | tf_op jit(solution)/shard_map/all_to_all | solution.py:95
  200.9 7.2 %all-to-all-done.2 = f32[16,1,128]{2,1,0:T(1,128)S(1)} async-done(((f32[16,1,128]{2,1,0:T(1,128)}), f32[16,1,128]{2,1,0:T(1,128)S(1)}, u32[]{:S(2)}, u32[]{:S(2)}) %all-to-all-start.2) | async-done | bytes 8224 | tf_op jit(solution)/shard_map/all_to_all | solution.py:131
  213.7 72.2 %while.46 = (s32[]{:T(128)}, bf16[4,576,512]{2,1,0:T(8,128)(2,1)}, f32[32,64,1024]{2,1,0:T(8,128)}, f32[4,64,1024]{2,0,1:T(4,128)}, bf16[4,64,1024]{2,1,0:T(8,12...) while((s32[]{:T(128)}, bf16[4,576,512]{2,1,0:T(8,128)(2,1)}, ...), condition=%wide.region_21.22_spmd.clone, body=%wide.region_19.21_spmd.clone.sunk | while | flops 1212022784 | bytes 40981276 | solution.py:174
  220.5 5.1 %scatter_fusion = f32[32,64,1024]{2,1,0:T(8,128)} fusion(f32[32,64,1024]{2,1,0:T(8,128)} %get-tuple-element.624, s32[8]{0:T(128)S(1)} %fusion.79, f32[8,64,1024]{2,1,0:T(8,128)} %bitcast.138), kind=kCustom, calls=%fused_computation.5.clone.clone.1 | custom fusion | flops 524288 | bytes 6291488 | tf_op jit(solution)/shard_map/while/body/eval_jaxpr/scatter-add | solution.py:163
  225.9 5.8 %dynamic_update_slice.51 = f32[4,64,1024]{2,0,1:T(4,128)} dynamic-update-slice(f32[4,64,1024]{2,0,1:T(4,128)} %get-tuple-element.625, f32[1,64,1024]{2,0,1:T(1,128)S(1)} %copy.96, s32[]{:T(128)} %get-tuple-element.622, s32[]{:T(128)} %constant.189.clone.1..sunk.2, s32[]{:T(128)} %constant.189.clone.1..sunk.2) | dynamic-update-slice | bytes 524292 | tf_op jit(solution)/shard_map/while/body/eval_jaxpr/jit(dynamic_update_index_in_dim)/dynamic_update_slice | solution.py:159
  238.5 5.1 %scatter_fusion = f32[32,64,1024]{2,1,0:T(8,128)} fusion(f32[32,64,1024]{2,1,0:T(8,128)} %get-tuple-element.624, s32[8]{0:T(128)S(1)} %fusion.79, f32[8,64,1024]{2,1,0:T(8,128)} %bitcast.138), kind=kCustom, calls=%fused_computation.5.clone.clone.1 | custom fusion | flops 524288 | bytes 6291488 | tf_op jit(solution)/shard_map/while/body/eval_jaxpr/scatter-add | solution.py:163
  244.0 5.8 %dynamic_update_slice.51 = f32[4,64,1024]{2,0,1:T(4,128)} dynamic-update-slice(f32[4,64,1024]{2,0,1:T(4,128)} %get-tuple-element.625, f32[1,64,1024]{2,0,1:T(1,128)S(1)} %copy.96, s32[]{:T(128)} %get-tuple-element.622, s32[]{:T(128)} %constant.189.clone.1..sunk.2, s32[]{:T(128)} %constant.189.clone.1..sunk.2) | dynamic-update-slice | bytes 524292 | tf_op jit(solution)/shard_map/while/body/eval_jaxpr/jit(dynamic_update_index_in_dim)/dynamic_update_slice | solution.py:159
  256.6 5.2 %scatter_fusion = f32[32,64,1024]{2,1,0:T(8,128)} fusion(f32[32,64,1024]{2,1,0:T(8,128)} %get-tuple-element.624, s32[8]{0:T(128)S(1)} %fusion.79, f32[8,64,1024]{2,1,0:T(8,128)} %bitcast.138), kind=kCustom, calls=%fused_computation.5.clone.clone.1 | custom fusion | flops 524288 | bytes 6291488 | tf_op jit(solution)/shard_map/while/body/eval_jaxpr/scatter-add | solution.py:163
  262.1 5.8 %dynamic_update_slice.51 = f32[4,64,1024]{2,0,1:T(4,128)} dynamic-update-slice(f32[4,64,1024]{2,0,1:T(4,128)} %get-tuple-element.625, f32[1,64,1024]{2,0,1:T(1,128)S(1)} %copy.96, s32[]{:T(128)} %get-tuple-element.622, s32[]{:T(128)} %constant.189.clone.1..sunk.2, s32[]{:T(128)} %constant.189.clone.1..sunk.2) | dynamic-update-slice | bytes 524292 | tf_op jit(solution)/shard_map/while/body/eval_jaxpr/jit(dynamic_update_index_in_dim)/dynamic_update_slice | solution.py:159
  274.7 5.1 %scatter_fusion = f32[32,64,1024]{2,1,0:T(8,128)} fusion(f32[32,64,1024]{2,1,0:T(8,128)} %get-tuple-element.624, s32[8]{0:T(128)S(1)} %fusion.79, f32[8,64,1024]{2,1,0:T(8,128)} %bitcast.138), kind=kCustom, calls=%fused_computation.5.clone.clone.1 | custom fusion | flops 524288 | bytes 6291488 | tf_op jit(solution)/shard_map/while/body/eval_jaxpr/scatter-add | solution.py:163
  280.1 5.8 %dynamic_update_slice.51 = f32[4,64,1024]{2,0,1:T(4,128)} dynamic-update-slice(f32[4,64,1024]{2,0,1:T(4,128)} %get-tuple-element.625, f32[1,64,1024]{2,0,1:T(1,128)S(1)} %copy.96, s32[]{:T(128)} %get-tuple-element.622, s32[]{:T(128)} %constant.189.clone.1..sunk.2, s32[]{:T(128)} %constant.189.clone.1..sunk.2) | dynamic-update-slice | bytes 524292 | tf_op jit(solution)/shard_map/while/body/eval_jaxpr/jit(dynamic_update_index_in_dim)/dynamic_update_slice | solution.py:159
  285.9 28.3 %while.45 = (s32[]{:T(128)}, bf16[4,512,1024]{2,1,0:T(8,128)(2,1)}, bf16[4,576,512]{2,1,0:T(8,128)(2,1)}, s32[4]{0:T(128)S(1)}, bf16[4,64,1024]{2,1,0:T(8,128)(2...) while((s32[]{:T(128)}, bf16[4,512,1024]{2,1,0:T(8,128)(2,1)}, ...), condition=%wide.region_23.24_spmd, body=%wide.region_22.23_spmd.sunk | while | flops 604569600 | bytes 8586387 | solution.py:183
  318.3 6.3 %copy.71 = bf16[16,2,64,1024]{3,1,2,0:T(2,128)(2,1)} copy(bf16[16,2,64,1024]{3,2,1,0:T(8,128)(2,1)S(1)} %bitcast.142) | data formatting | bytes 8388608 | tf_op jit(solution)/shard_map/reshape | solution.py:190
  324.6 4.7 %all-to-all-start.3 = ((bf16[16,2,64,1024]{3,1,2,0:T(2,128)(2,1)}), bf16[16,2,64,1024]{3,1,2,0:T(2,128)(2,1)}, u32[]{:S(2)}, u32[]{:S(2)}) async-start(bf16[16,2,64,1024]{3,1,2,0:T(2,128)(2,1)} %copy.71), calls=%async_computation.4 | async-start | bytes 8388608 | tf_op jit(solution)/shard_map/all_to_all | solution.py:189
  330.5 108.9 %psum.15 = f32[]{:T(128)} all-reduce(f32[]{:T(128)S(6)} %add.200), channel_id=1, replica_groups=mesh['dp'=16,'inner'=8] {'dp','inner'}, use_global_device_ids=true, to_apply=%region_18.19 | all-reduce | flops 1 | bytes 8 | tf_op jit(solution)/shard_map/psum | solution.py:129
  440.1 4.8 %fusion.27 = bf16[4,64,1024]{2,0,1:T(4,128)(2,1)S(1)} fusion(f32[4,64,1024]{2,0,1:T(4,128)S(1)} %copy-done.3, bf16[16,2,64,1024]{3,1,2,0:T(2,128)(2,1)} %all-to-all-done.3, s32[16,2]{0,1:T(2,128)S(1)} %get-tuple-element.386, pred[16,2]{0,1:T(4,128)(4,1)S(1)} %get-tuple-element.382), kind=kOutput, calls=%fused_computation.52 | convolution fusion | flops 17301760 | bytes 5767328 | tf_op jit(solution)/shard_map/eg,ecd->gcd/dot_general | solution.py:196
  (222 shorter events, 99.6 us)
Async XLA Ops:
  7.2 5.7 %copy-start = (bf16[4,64,1024]{2,1,0:T(8,128)(2,1)S(1)}, bf16[4,64,1024]{2,1,0:T(8,128)(2,1)}, u32[]{:S(2)}) copy-start(bf16[4,64,1024]{2,1,0:T(8,128)(2,1)} %param.10) | copy-start | bytes 1572868
  7.2 5.7 %copy-start.2 = (bf16[4,64,1024]{2,1,0:T(8,128)(2,1)S(1)}, bf16[4,64,1024]{2,1,0:T(8,128)(2,1)}, u32[]{:S(2)}) copy-start(bf16[4,64,1024]{2,1,0:T(8,128)(2,1)} %param.9) | copy-start | bytes 1572868
  7.2 76.2 %all-gather.3.cloned.1.call-start = ((), (), s32[]{:S(2)}) async-start(), calls=%async_computation.5 | async-start | bytes 8912896 | tf_op jit(solution)/shard_map/all_gather | solution.py:50
  7.9 109.2 %all-gather.5.cloned.1.call-start = ((), (), s32[]{:S(2)}) async-start(), calls=%async_computation.6 | async-start | bytes 4718592 | tf_op jit(solution)/shard_map/all_gather | solution.py:54
  146.5 33.5 %all-to-all-start.1 = ((f32[16,1,128]{2,1,0:T(1,128)}), f32[16,1,128]{2,1,0:T(1,128)S(1)}, u32[]{:S(2)}, u32[]{:S(2)}) async-start(f32[16,1,128]{2,1,0:T(1,128)} %reshape.334), calls=%async_computation.1 | async-start | bytes 16384 | tf_op jit(solution)/shard_map/all_to_all | solution.py:102
  180.0 14.2 %all-to-all-start = ((f32[16,1,128]{2,1,0:T(1,128)}), f32[16,1,128]{2,1,0:T(1,128)S(1)}, u32[]{:S(2)}, u32[]{:S(2)}) async-start(f32[16,1,128]{2,1,0:T(1,128)} %reshape.332), calls=%async_computation | async-start | bytes 16384 | tf_op jit(solution)/shard_map/all_to_all | solution.py:95
  197.1 10.9 %all-to-all-start.2 = ((f32[16,1,128]{2,1,0:T(1,128)}), f32[16,1,128]{2,1,0:T(1,128)S(1)}, u32[]{:S(2)}, u32[]{:S(2)}) async-start(f32[16,1,128]{2,1,0:T(1,128)} %reshape.336), calls=%async_computation.2 | async-start | bytes 16384 | tf_op jit(solution)/shard_map/all_to_all | solution.py:131
  200.6 245.3 %reduce-scatter.2.cloned.1.call-start = ((), (), s32[]{:S(2)}) async-start(), calls=%async_computation.7 | async-start | bytes 4718592 | tf_op jit(solution)/shard_map/reduce_scatter | solution.py:182
  213.7 2.5 copy-start.1
  231.8 2.5 copy-start.1
  249.8 2.5 copy-start.1
  267.9 2.5 copy-start.1
  324.6 115.5 %copy-start.3 = (f32[4,64,1024]{2,0,1:T(4,128)S(1)}, f32[4,64,1024]{2,0,1:T(4,128)}, u32[]{:S(2)}) copy-start(f32[4,64,1024]{2,0,1:T(4,128)} %get-tuple-element.278) | copy-start | bytes 3145732
  324.6 115.5 %all-to-all-start.3 = ((bf16[16,2,64,1024]{3,1,2,0:T(2,128)(2,1)}), bf16[16,2,64,1024]{3,1,2,0:T(2,128)(2,1)}, u32[]{:S(2)}, u32[]{:S(2)}) async-start(bf16[16,2,64,1024]{3,1,2,0:T(2,128)(2,1)} %copy.71), calls=%async_computation.4 | async-start | bytes 8388608 | tf_op jit(solution)/shard_map/all_to_all | solution.py:189
Sparse Core Ops, SparseCore 0:
  10.1 73.1 all-gather.2
  85.1 31.9 all-gather.4
  314.4 33.7 reduce-scatter.1
where the time goes:
time: 456 us; the launch traced here: 453 us
  blocking collectives  135 us (30%)
  waiting for transfers between devices  108 us (24%)
  local copies, waits for them, and re-layouts  82.3 us (18%)
  matrix products  37 us (8%)
  other arithmetic  36.1 us (8%)
  starting transfers between devices  21.9 us (5%)
  between operations  17.2 us (4%)
  loops' own time  16.1 us (4%)
    psum x1, blocking collectives, body(): lax.psum(local_loss, ('dp', 'inner'))  109 us
    all_gather x1, waiting for transfers between devices, body(): shard_rows = lax.all_gather(passages, 'dp', axis=0, tiled=True)  70.1 us
    dynamic_update_slice x8, local copies, waits for them, and re-layouts, backward(): lax.dynamic_update_index_in_dim(own_grad, passage_part[:slice_rows], bloc...  24.4 us
    all_gather x1, waiting for transfers between devices, body(): whole_queries = lax.all_gather(queries, 'inner', axis=1, tiled=True)  23.1 us
    scatter-add x4, other arithmetic, backward(): slot_grad.at[slot_targets]  20.5 us
    dot_general x8, matrix products, scores(): jnp.einsum('cd,rd->cr', candidates(block_index), query_block, preferred_e...  16.6 us
    squeeze x12, local copies, waits for them, and re-layouts, candidates(): lax.dynamic_index_in_dim(negatives, block_index, 0, keepdims=False)  16.3 us
    pmax x1, blocking collectives, body(): peak_all = lax.pmax(row_peak, 'inner')  13.3 us
  transfers between devices with their start and end apart: 7, of which 4 were waited for; matrix products, arithmetic and copies ran while one was open for 7% of the time, Pallas kernels for 0%

commit v1 on v0

v1 whole, which is shorter than its diff:
```python
import functools
import math

import jax
import jax.numpy as jnp
from jax import lax
from jax.experimental import pallas as pl
from jax.experimental.pallas import tpu as pltpu
from jax.sharding import PartitionSpec as P

MESH = pl.DeviceIdType.MESH
NEG = -1e30
SIDE = 4
CAP = 2
VMEM_LIMIT = 60 * 1024 * 1024

VM = pl.BlockSpec(memory_space=pltpu.VMEM)
SM = pl.BlockSpec(memory_space=pltpu.SMEM)


def mod4(v):
    return lax.rem(v + SIDE, SIDE)


class Place:
    def __init__(self):
        self.dp = lax.axis_index("dp")
        self.inner = lax.axis_index("inner")
        self.y, self.x = self.dp // SIDE, lax.rem(self.dp, SIDE)
        self.z, self.c = self.inner // 2, lax.rem(self.inner, 2)

    def move(self, axis, step):
        if axis == "x":
            return (self.y * SIDE + mod4(self.x + step), self.inner)
        if axis == "y":
            return (mod4(self.y + step) * SIDE + self.x, self.inner)
        if axis == "z":
            return (self.dp, mod4(self.z + step) * 2 + self.c)
        return (self.dp, self.z * 2 + (1 - self.c))

    def group(self, first, rf, rt):
        if first == "y":
            return mod4(self.y + rf) * SIDE + mod4(self.x + rt)
        return mod4(self.y + rt) * SIDE + mod4(self.x + rf)


class Copies:
    def __init__(self, send_sem, recv_sem):
        self.send_sem, self.recv_sem, self.count, self.made = send_sem, recv_sem, 0, []

    def send(self, src, dst, device, landing=None):
        i = self.count
        self.count += 1
        copy = pltpu.make_async_remote_copy(
            src_ref=src, dst_ref=dst, send_sem=self.send_sem.at[i], recv_sem=self.recv_sem.at[i],
            device_id=device, device_id_type=MESH)
        copy.start()
        self.made.append(copy)
        if landing is None:
            return copy
        return pltpu.make_async_remote_copy(
            src_ref=src, dst_ref=landing, send_sem=self.send_sem.at[i],
            recv_sem=self.recv_sem.at[i], device_id=device, device_id_type=MESH)

    def drain(self):
        for copy in self.made:
            copy.wait_send()


def meet(devices):
    barrier = pltpu.get_barrier_semaphore()
    for device in devices:
        pl.semaphore_signal(barrier, inc=1, device_id=device, device_id_type=MESH)
    pl.semaphore_wait(barrier, len(devices))


def neighbours(me):
    return [me.move(a, s) for a in "xyz" for s in (1, -1)] + [me.move("core", 0)]


HALVES = (("y", "x"), ("x", "y"))


def gather_kernel(table, q_ref, p_ref, full_ref, got_ref, *scratch):
    near = [(None,) + scratch[3 * h:3 * h + 3] for h in (0, 1)]
    stage, relay, send_sem, recv_sem, local_sem = scratch[6:]
    me = Place()
    per, rows = p_ref.shape[0], p_ref.shape[1]
    half = rows // 2
    two = per // 2
    meet(neighbours(me))
    net = Copies(send_sem, recv_sem)
    mine = [p_ref.at[:, pl.ds(h * half, half)] for h in (0, 1)]

    first = []
    for h, (f, t) in enumerate(HALVES):
        up = net.send(mine[h], near[h][3], me.move(f, 1))
        down = net.send(mine[h], near[h][1], me.move(f, -1))
        first.append((up, down))
    at = lambda z, c: full_ref.at[mod4(z) * 2 + c]
    own_slot = at(me.z, me.c)
    z_up = net.send(q_ref, own_slot, me.move("z", 1), at(me.z - 1, me.c))
    z_down = net.send(q_ref, own_slot, me.move("z", -1), at(me.z + 1, me.c))
    pair = [net.send(q_ref, own_slot, me.move("core", 0), at(me.z, 1 - me.c))]
    keep = pltpu.make_async_copy(q_ref, own_slot, local_sem)
    keep.start()

    arrivals = []
    relays = []

    def spread(h, rf):
        f, t = HALVES[h]
        source = me.group(f, rf, 0)
        for dt in range(SIDE):
            if dt == 0 and rf == 0:
                continue
            group = me.group(f, 0, dt)
            for c in range(CAP):
                pick = table[group, source * CAP + c]
                if rf == 0:
                    block = p_ref[pick, pl.ds(h * half, half)]
                else:
                    block = near[h][rf][pick]
                if dt == 0:
                    got_ref[h, rf * CAP + c] = block
                else:
                    stage[h, dt, rf, c] = block
        up, down = me.move(t, 1), me.move(t, -1)
        a = net.send(stage.at[h, 2, rf, 0], relay.at[h, 0, rf], up)
        b = net.send(stage.at[h, 2, rf, 1], relay.at[h, 1, rf], down)
        relays.append((h, rf, a, b))
        slots = pl.ds
        arrivals.append(net.send(stage.at[h, 1, rf], got_ref.at[h, slots(24 + rf * CAP, CAP)], up))
        arrivals.append(net.send(stage.at[h, 3, rf], got_ref.at[h, slots(8 + rf * CAP, CAP)], down))

    def pass_on(entry):
        h, rf, a, b = entry
        t = HALVES[h][1]
        a.wait_recv()
        arrivals.append(net.send(relay.at[h, 0, rf], got_ref.at[h, 16 + rf * CAP], me.move(t, 1)))
        b.wait_recv()
        arrivals.append(
            net.send(relay.at[h, 1, rf], got_ref.at[h, 16 + rf * CAP + 1], me.move(t, -1)))

    for h in (0, 1):
        spread(h, 0)
        got_ref[h, 0:CAP] = jnp.zeros((CAP,) + got_ref.shape[2:], got_ref.dtype)
    second = []
    for h, (f, t) in enumerate(HALVES):
        up, down = first[h]
        up.wait_recv()
        a = net.send(near[h][3].at[0:two], near[h][2].at[0:two], me.move(f, 1))
        down.wait_recv()
        b = net.send(near[h][1].at[two:per], near[h][2].at[two:per], me.move(f, -1))
        second.append((a, b))
    for h in (0, 1):
        spread(h, 1)
        spread(h, 3)
    z_up.wait_recv()
    behind, ahead = at(me.z - 1, me.c), at(me.z + 1, me.c)
    across = mod4(me.z + 2) * 2
    far = full_ref.at[across + me.c]
    za = net.send(behind.at[0:two], behind.at[0:two], me.move("z", 1), far.at[0:two])
    pair.append(net.send(behind, behind, me.move("core", 0), at(me.z - 1, 1 - me.c)))
    z_down.wait_recv()
    zb = net.send(ahead.at[two:per], ahead.at[two:per], me.move("z", -1), far.at[two:per])
    pair.append(net.send(ahead, ahead, me.move("core", 0), at(me.z + 1, 1 - me.c)))
    for entry in relays[:2]:
        pass_on(entry)
    for h in (0, 1):
        for copy in second[h]:
            copy.wait_recv()
        spread(h, 2)
    za.wait_recv()
    zb.wait_recv()
    pair.append(net.send(far, far, me.move("core", 0), full_ref.at[across + 1 - me.c]))
    for entry in relays[2:]:
        pass_on(entry)
    for copy in pair + arrivals:
        copy.wait_recv()
    keep.wait()
    net.drain()


def slot_pair(rank, lists, dp, b, k):
    block = lists[dp * SIDE + b, k]
    group = block // SIDE
    r = rank[dp, block]
    ry = mod4(group // SIDE - dp // SIDE)
    rx = mod4(lax.rem(group, SIDE) - lax.rem(dp, SIDE))
    return block, rx * 8 + ry * 2 + r, ry * 8 + rx * 2 + r


def load_candidates(where, rank, lists, b, p_ref, got_ref, cand):
    dp = where[0]
    rows = p_ref.shape[1]
    half = rows // 2
    picks = lists.shape[1]
    cand[0:rows] = p_ref[b]
    for k in range(picks):
        _, sa, sb = slot_pair(rank, lists, dp, b, k)
        base = rows * (k + 1)
        cand[base:base + half] = got_ref[0, sa]
        cand[base + half:base + rows] = got_ref[1, sb]


def forward_kernel(where, rank, lists, p_ref, got_ref, full_ref, logit_ref, row_ref, dense_ref,
                   own_ref, cand):
    dp, inner = where[0], where[1]
    per, rows, width = p_ref.shape
    picks = lists.shape[1]
    queries = full_ref.shape[0] * rows
    scale = 1.0 / math.sqrt(width)
    dense_ref[...] = jnp.full(dense_ref.shape, NEG, jnp.float32)
    own_ref[...] = jnp.zeros(own_ref.shape, jnp.float32)
    lane = lax.broadcasted_iota(jnp.int32, (rows, 128), 1)
    sub = lax.broadcasted_iota(jnp.int32, (rows, 128), 0)
    lane1 = lax.broadcasted_iota(jnp.int32, (1, 128), 1)
    wide_lane = lax.broadcasted_iota(jnp.int32, (rows, queries), 1)
    wide_sub = lax.broadcasted_iota(jnp.int32, (rows, queries), 0)

    def step(b, carry):
        load_candidates(where, rank, lists, b, p_ref, got_ref, cand)
        q = full_ref[:, b].reshape(queries, width)
        logit_ref[b] = lax.dot_general(
            cand[...], q, (((1,), (1,)), ((), ())), preferred_element_type=jnp.float32) * scale
        peak = jnp.full((1, queries), NEG, jnp.float32)
        for i in range(picks + 1):
            part = logit_ref[b, i * rows:(i + 1) * rows]
            peak = jnp.maximum(peak, jnp.max(part, axis=0, keepdims=True))
            top = jnp.max(part, axis=1, keepdims=True)
            mass = jnp.sum(jnp.exp(part - top), axis=1, keepdims=True)
            lse = top + jnp.log(mass)
            if i == 0:
                block = dp * SIDE + b
                hit = wide_lane == wide_sub + inner * rows
                own_ref[...] += jnp.sum(jnp.where(hit, part, 0.0))
            else:
                block = lists[dp * SIDE + b, i - 1]
            side = block // 32
            line = lax.rem(block, 32)
            row = jnp.sum(jnp.where(lane == sub + side * 64, lse, 0.0), axis=0, keepdims=True)
            old = dense_ref[pl.ds(line, 1)]
            high = jnp.maximum(old, row)
            joined = high + jnp.log(jnp.exp(old - high) + jnp.exp(row - high))
            dense_ref[pl.ds(line, 1)] = jnp.where(lane1 // 64 == side, joined, old)
        total = jnp.zeros((1, queries), jnp.float32)
        for i in range(picks + 1):
            part = logit_ref[b, i * rows:(i + 1) * rows]
            total = total + jnp.sum(jnp.exp(part - peak), axis=0, keepdims=True)
        row_ref[pl.ds(b, 1)] = peak + jnp.log(total)
        return carry

    lax.fori_loop(0, per, step, 0)


def stats_kernel(groups, inners, rows_per, row_in, dense_in, own_in, row_out, dense_out, loss_out,
                 all_rows, all_dense, send_sem, recv_sem):
    me = Place()
    peers = [("dp", o) for o in range(1, groups)] + [("inner", o) for o in range(1, inners)]

    def peer(kind, o):
        if kind == "dp":
            return (lax.rem(me.dp + o, groups), me.inner)
        return (me.dp, lax.rem(me.inner + o, inners))

    meet([peer(*p) for p in peers])
    net = Copies(send_sem, recv_sem)
    waits = []
    for kind, o in peers:
        if kind == "dp":
            origin = lax.rem(me.dp - o + groups, groups)
            waits.append(net.send(dense_in, all_dense.at[me.dp], peer(kind, o),
                                  all_dense.at[origin]))
        else:
            origin = lax.rem(me.inner - o + inners, inners)
            waits.append(net.send(row_in, all_rows.at[me.inner], peer(kind, o),
                                  all_rows.at[origin]))
    all_dense[me.dp] = dense_in[...]
    all_rows[me.inner] = row_in[...]
    for copy in waits:
        copy.wait_recv()

    def fold(ref):
        top = jnp.max(ref[...], axis=0)
        return top + jnp.log(jnp.sum(jnp.exp(ref[...] - top[None]), axis=0))

    rows = fold(all_rows)
    dense = fold(all_dense)
    row_out[...] = rows
    dense_out[...] = dense
    lane = lax.broadcasted_iota(jnp.int32, rows.shape, 1)
    mine = jnp.sum(jnp.where(lane // rows_per == me.inner, rows, 0.0))
    line = lax.broadcasted_iota(jnp.int32, dense.shape, 0)
    side = lax.broadcasted_iota(jnp.int32, dense.shape, 1) // 64
    owned = (line + 32 * side) // SIDE == me.dp
    mine = mine + jnp.sum(jnp.where(owned, dense, 0.0))
    loss_out[...] = mine - 2.0 * own_in[...]
    net.drain()


def backward_kernel(where, rank, lists, p_ref, got_ref, full_ref, logit_ref, row_ref, dense_ref,
                    part_ref, query_ref, own_ref, cand, weight, prod, total):
    dp, inner = where[0], where[1]
    per, rows, width = p_ref.shape
    half = rows // 2
    picks = lists.shape[1]
    shards = full_ref.shape[0]
    queries = shards * rows
    lane = lax.broadcasted_iota(jnp.int32, (rows, 128), 1)
    sub = lax.broadcasted_iota(jnp.int32, (rows, 128), 0)
    wide_lane = lax.broadcasted_iota(jnp.int32, (rows, queries), 1)
    wide_sub = lax.broadcasted_iota(jnp.int32, (rows, queries), 0)

    def clear(i, carry):
        for h in (0, 1):
            total[h, i] = jnp.zeros(total.shape[2:], jnp.float32)
        return carry

    lax.fori_loop(0, total.shape[1], clear, 0)

    def step(b, carry):
        load_candidates(where, rank, lists, b, p_ref, got_ref, cand)
        q = full_ref[:, b].reshape(queries, width)
        row = row_ref[pl.ds(b, 1)]
        for i in range(picks + 1):
            block = dp * SIDE + b if i == 0 else lists[dp * SIDE + b, i - 1]
            line = dense_ref[pl.ds(lax.rem(block, 32), 1)]
            col = jnp.sum(jnp.where(lane == sub + (block // 32) * 64, line, 0.0), axis=1,
                          keepdims=True)
            part = logit_ref[b, i * rows:(i + 1) * rows]
            probs = 0.5 * jnp.exp(part - row) + 0.5 * jnp.exp(part - col)
            if i == 0:
                probs = probs - jnp.where(wide_lane == wide_sub + inner * rows, 1.0, 0.0)
            weight[i * rows:(i + 1) * rows] = probs.astype(jnp.bfloat16)
        prod[...] = jnp.dot(weight[...], q, preferred_element_type=jnp.float32)
        own_ref[b] = prod[0:rows]
        for k in range(picks):
            _, sa, sb = slot_pair(rank, lists, dp, b, k)
            base = rows * (k + 1)
            total[0, sa] = total[0, sa] + prod[base:base + half]
            total[1, sb] = total[1, sb] + prod[base + half:base + rows]
        grad = lax.dot_general(weight[...], cand[...], (((0,), (0,)), ((), ())),
                               preferred_element_type=jnp.float32)
        query_ref[:, b] = grad.astype(jnp.bfloat16).reshape(shards, rows, width)
        return carry

    lax.fori_loop(0, per, step, 0)

    def finish(i, carry):
        for h in (0, 1):
            part_ref[h, i] = total[h, i].astype(jnp.bfloat16)
        return carry

    lax.fori_loop(0, total.shape[1], finish, 0)


def reduce_kernel(groups, inners, count, rank, part_ref, query_ref, own_ref, loss_in, loss_out,
                  qg_ref, pg_ref, *scratch):
    bank = 2 * (SIDE - 1) * SIDE
    seen = [[scratch[(h * 3 + st) * SIDE:(h * 3 + st + 1) * SIDE] for st in range(3)]
            for h in (0, 1)]
    (relay, dense, merge, last, pair_in, qsum, zmerge, zlast, loss_dp, loss_inner, loss_mid,
     send_sem, recv_sem) = scratch[bank:]
    me = Place()
    per, rows, width = own_ref.shape
    half, two = rows // 2, per // 2
    f32, b16 = jnp.float32, jnp.bfloat16

    def loss_peer(kind, o):
        if kind == "dp":
            return (lax.rem(me.dp + o, groups), me.inner)
        return (me.dp, lax.rem(me.inner + o, inners))

    def dp_offset(o):
        return loss_peer("dp", o)

    def inner_offset(o):
        return loss_peer("inner", o)

    meet([dp_offset(o) for o in range(1, groups)] + [inner_offset(o) for o in range(1, inners)])
    net = Copies(send_sem, recv_sem)

    relays, parts = [], {}
    for rf in (2, 1, 3, 0):
        for h, (f, t) in enumerate(HALVES):
            up, down = me.move(t, 1), me.move(t, -1)
            a = net.send(part_ref.at[h, 16 + rf * CAP], relay.at[h, 0, rf], up)
            b = net.send(part_ref.at[h, 16 + rf * CAP + 1], relay.at[h, 1, rf], down)
            relays.append((h, rf, a, b))
            parts[h, rf] = [
                net.send(part_ref.at[h, pl.ds(8 + rf * CAP, CAP)], seen[h][2][rf], up),
                net.send(part_ref.at[h, pl.ds(24 + rf * CAP, CAP)], seen[h][0][rf], down)]
        if rf == 2:
            swaps = {}
            for dz in (2, 1, 3, 0):
                swaps[dz] = net.send(query_ref.at[mod4(me.z + dz) * 2 + 1 - me.c],
                                     pair_in.at[dz], me.move("core", 0))
            loss_waits = [
                net.send(loss_in, loss_dp.at[me.dp], dp_offset(o),
                         loss_dp.at[lax.rem(me.dp - o + groups, groups)])
                for o in range(1, groups)]
            loss_dp[me.dp] = loss_in[...]

    def pass_on(entry):
        h, rf, a, b = entry
        t = HALVES[h][1]
        a.wait_recv()
        parts[h, rf].append(net.send(relay.at[h, 0, rf], seen[h][1][rf].at[0], me.move(t, 1)))
        b.wait_recv()
        parts[h, rf].append(net.send(relay.at[h, 1, rf], seen[h][1][rf].at[1], me.move(t, -1)))

    def join(dz):
        swaps[dz].wait_recv()
        slot = mod4(me.z + dz) * 2 + me.c

        def body(j, carry):
            both = query_ref[slot, j].astype(f32) + pair_in[dz, j].astype(f32)
            qsum[dz, j] = both.astype(b16)
            return carry

        lax.fori_loop(0, per, body, 0)

    join(2)
    za = net.send(qsum.at[2, 0:two], zmerge.at[0], me.move("z", 1))
    zb = net.send(qsum.at[2, two:per], zmerge.at[1], me.move("z", -1))
    for entry in relays[:2]:
        pass_on(entry)
    join(1)
    join(3)

    def fold_in(target, rd, source, start):
        def body(j, carry):
            both = target[rd, start + j].astype(f32) + source[j].astype(f32)
            target[rd, start + j] = both.astype(b16)
            return carry

        lax.fori_loop(0, two, body, 0)

    za.wait_recv()
    fold_in(qsum, 1, zmerge.at[0], 0)
    z_up = net.send(qsum.at[1], zlast.at[0], me.move("z", 1))
    zb.wait_recv()
    fold_in(qsum, 3, zmerge.at[1], two)
    z_down = net.send(qsum.at[3], zlast.at[1], me.move("z", -1))
    for copy in loss_waits:
        copy.wait_recv()
    mid = jnp.sum(loss_dp[...], axis=0)
    loss_mid[...] = mid
    loss_waits = [
        net.send(loss_mid, loss_inner.at[me.inner], inner_offset(o),
                 loss_inner.at[lax.rem(me.inner - o + inners, inners)])
        for o in range(1, inners)]
    loss_inner[me.inner] = mid

    def collect(h, rf):
        f, t = HALVES[h]
        for copy in parts[h, rf]:
            copy.wait_recv()
        owner = me.group(f, rf, 0)
        for j in range(per):
            acc = jnp.zeros((half, width), f32)
            for st in range(SIDE):
                if st == 0 and rf == 0:
                    continue
                r = rank[me.group(f, 0, st), owner * per + j]
                live = (r >= 0).astype(f32)
                c = jnp.maximum(r, 0)
                if st == 0:
                    block = part_ref[h, rf * CAP + c]
                else:
                    block = seen[h][st - 1][rf][c]
                acc = acc + block.astype(f32) * live
            if rf == 0:
                own = own_ref[j, h * half:(h + 1) * half]
                own_ref[j, h * half:(h + 1) * half] = own + acc
            else:
                dense[h, rf, j] = acc.astype(b16)

    for h, (f, t) in enumerate(HALVES):
        collect(h, 2)
        merges = [net.send(dense.at[h, 2, 0:two], merge.at[h, 0], me.move(f, 1)),
                  net.send(dense.at[h, 2, two:per], merge.at[h, 1], me.move(f, -1))]
        parts[h, "merge"] = merges
    for entry in relays[2:6]:
        pass_on(entry)
    ends = []
    for h, (f, t) in enumerate(HALVES):
        for rf, slot in ((1, 0), (3, 1)):
            collect(h, rf)
            parts[h, "merge"][slot].wait_recv()
            fold_in(dense.at[h], rf, merge.at[h, slot], slot * two)
            ends.append(net.send(dense.at[h, rf], last.at[h, slot],
                                 me.move(f, 1 if slot == 0 else -1)))
    for entry in relays[6:]:
        pass_on(entry)
    join_final = swaps[0]
    join_final.wait_recv()
    z_up.wait_recv()
    z_down.wait_recv()
    own_slot = me.z * 2 + me.c

    def finish_query(j, carry):
        both = query_ref[own_slot, j].astype(f32) + pair_in[0, j].astype(f32)
        both = both + zlast[0, j].astype(f32) + zlast[1, j].astype(f32)
        qg_ref[j] = both.astype(b16)
        return carry

    lax.fori_loop(0, per, finish_query, 0)
    for copy in loss_waits:
        copy.wait_recv()
    loss_out[...] = jnp.sum(loss_inner[...], axis=0) * (1.0 / count)
    for h in (0, 1):
        collect(h, 0)
    for copy in ends:
        copy.wait_recv()
    for h in (0, 1):
        def finish(j, carry, h=h):
            span = pl.ds(h * half, half)
            both = own_ref[j, span] + last[h, 0, j].astype(f32) + last[h, 1, j].astype(f32)
            pg_ref[j, span] = both.astype(b16)
            return carry

        lax.fori_loop(0, per, finish, 0)
    net.drain()


def params(cid=None):
    if cid is None:
        return pltpu.CompilerParams(vmem_limit_bytes=VMEM_LIMIT)
    return pltpu.CompilerParams(vmem_limit_bytes=VMEM_LIMIT, collective_id=cid,
                                has_side_effects=True)


def sems(n):
    return [pltpu.SemaphoreType.DMA((n,)), pltpu.SemaphoreType.DMA((n,))]


def tables(neg_lists, groups, per):
    blocks = neg_lists.shape[0]
    ids = jnp.arange(blocks, dtype=jnp.int32)
    lists = neg_lists.reshape(groups, -1)
    present = jnp.any(lists[:, :, None] == ids[None, None, :], axis=1)
    quads = present.reshape(groups, groups, per).astype(jnp.int32)
    earlier = (jnp.arange(per)[:, None] < jnp.arange(per)[None, :]).astype(jnp.int32)
    rank = jnp.sum(quads[:, :, :, None] * earlier[None, None], axis=2)
    rank = jnp.where(quads == 1, rank, -1)
    slot = jnp.arange(CAP, dtype=jnp.int32)
    local = jnp.arange(per, dtype=jnp.int32)
    block = jnp.sum(
        jnp.where(rank[..., None] == slot, local[None, None, :, None], 0), axis=2)
    return rank.reshape(groups, blocks), block.reshape(groups, groups * CAP)


def body(queries, passages, neg_lists):
    per, rows, width = queries.shape
    groups, inners = lax.axis_size("dp"), lax.axis_size("inner")
    picks = neg_lists.shape[1]
    half, two = rows // 2, per // 2
    slots = groups * CAP
    cands, full_rows = (picks + 1) * rows, rows * inners
    b16, f32 = jnp.bfloat16, jnp.float32
    sds = jax.ShapeDtypeStruct
    rank, block = tables(neg_lists, groups, per)
    where = jnp.stack([lax.axis_index("dp"), lax.axis_index("inner")]).astype(jnp.int32)

    full, got = pl.pallas_call(
        gather_kernel,
        out_shape=(sds((inners, per, rows, width), b16), sds((2, slots, half, width), b16)),
        in_specs=[SM, VM, VM], out_specs=(VM, VM),
        scratch_shapes=[
            pltpu.VMEM((per, half, width), b16) for _ in range(2 * (SIDE - 1))] + [
            pltpu.VMEM((2, SIDE, SIDE, CAP, half, width), b16),
            pltpu.VMEM((2, 2, SIDE, half, width), b16)] + sems(72) + [pltpu.SemaphoreType.DMA],
        compiler_params=params(0), name="gather",
    )(block, queries, passages)

    logits, row_lse, dense, own = pl.pallas_call(
        forward_kernel,
        out_shape=(sds((per, cands, full_rows), f32), sds((per, full_rows), f32),
                   sds((32, 128), f32), sds((8, 128), f32)),
        in_specs=[SM, SM, SM, VM, VM, VM], out_specs=(VM, VM, VM, VM),
        scratch_shapes=[pltpu.VMEM((cands, width), b16)],
        compiler_params=params(), name="forward",
    )(where, rank, neg_lists, passages, got, full)

    row_all, dense_all, loss = pl.pallas_call(
        functools.partial(stats_kernel, groups, inners, rows),
        out_shape=(sds((per, full_rows), f32), sds((32, 128), f32), sds((8, 128), f32)),
        in_specs=[VM, VM, VM], out_specs=(VM, VM, VM),
        scratch_shapes=[pltpu.VMEM((inners, per, full_rows), f32),
                        pltpu.VMEM((groups, 32, 128), f32)] + sems(24),
        compiler_params=params(1), name="stats",
    )(row_lse, dense, own)

    parts, qparts, own_grad = pl.pallas_call(
        backward_kernel,
        out_shape=(sds((2, slots, half, width), b16), sds((inners, per, rows, width), b16),
                   sds((per, rows, width), f32)),
        in_specs=[SM, SM, SM, VM, VM, VM, VM, VM, VM], out_specs=(VM, VM, VM),
        scratch_shapes=[
            pltpu.VMEM((cands, width), b16), pltpu.VMEM((cands, full_rows), b16),
            pltpu.VMEM((cands, width), f32), pltpu.VMEM((2, slots, half, width), f32)],
        compiler_params=params(), name="backward",
    )(where, rank, neg_lists, passages, got, full, logits, row_all, dense_all)

    loss_all, query_grad, passage_grad, _ = reduce_call(
        groups, inners, 2.0 * groups * per * full_rows, rank, parts, qparts, own_grad, loss)
    return (loss_all[0, 0], query_grad, passage_grad)


def reduce_call(groups, inners, count, rank, parts, qparts, own_grad, loss):
    per, rows, width = own_grad.shape
    half, two = rows // 2, per // 2
    b16, f32 = jnp.bfloat16, jnp.float32
    sds = jax.ShapeDtypeStruct

    def kernel(rank, part_ref, query_ref, own_in, loss_in, loss_out, qg_ref, pg_ref, own_ref,
               *scratch):
        own_ref[...] = own_in[...]
        reduce_kernel(groups, inners, count, rank, part_ref, query_ref, own_ref, loss_in, loss_out,
                      qg_ref, pg_ref, *scratch)

    return pl.pallas_call(
        kernel,
        out_shape=(sds((8, 128), f32), sds((per, rows, width), b16), sds((per, rows, width), b16),
                   sds((per, rows, width), f32)),
        in_specs=[SM, VM, VM, VM, VM], out_specs=(VM, VM, VM, VM),
        scratch_shapes=[
            pltpu.VMEM((CAP, half, width), b16) for _ in range(2 * (SIDE - 1) * SIDE)] + [
            pltpu.VMEM((2, 2, SIDE, half, width), b16),
            pltpu.VMEM((2, SIDE, per, half, width), b16),
            pltpu.VMEM((2, 2, two, half, width), b16),
            pltpu.VMEM((2, 2, per, half, width), b16),
            pltpu.VMEM((SIDE, per, rows, width), b16),
            pltpu.VMEM((SIDE, per, rows, width), b16),
            pltpu.VMEM((2, two, rows, width), b16),
            pltpu.VMEM((2, per, rows, width), b16),
            pltpu.VMEM((groups, 8, 128), f32),
            pltpu.VMEM((inners, 8, 128), f32),
            pltpu.VMEM((8, 128), f32)] + sems(96),
        compiler_params=params(2), name="reduce",
    )(rank, parts, qparts, own_grad, loss)


def solution(mesh):
    in_specs = (P("dp", "inner", None), P("dp", "inner", None), P())
    out_specs = (P(), P("dp", "inner", None), P("dp", "inner", None))
    return jax.shard_map(body, mesh=mesh, in_specs=in_specs, out_specs=out_specs, check_vma=False)
```

time: 456 us -> 140 us (0.31)
  blocking collectives: 135 us -> 0 us
  Pallas kernels: 0 us -> 131 us
  waiting for transfers between devices: 108 us -> 0 us
  local copies, waits for them, and re-layouts: 82.3 us -> 6.82 us
  matrix products: 37 us -> 0 us
  other arithmetic: 36.1 us -> 1.5 us
  starting transfers between devices: 21.9 us -> 0 us
  between operations: 17.2 us -> 0.7 us
  loops' own time: 16.1 us -> 0 us
    pallas_call x0 -> x5, Pallas kernels: none -> 131 us  [the longest x1 46.7 us: reduce_call(): pl.pallas_call(kernel, out_shape=(sds((8, 128), f32), sds((per, rows, wid...]
    psum x2 -> x0, blocking collectives: 122 us -> none  [the longest x1 109 us: body(): lax.psum(local_loss, ('dp', 'inner'))]
    all_gather x2 -> x0, waiting for transfers between devices: 93.2 us -> none  [the longest x1 70.1 us: body(): shard_rows = lax.all_gather(passages, 'dp', axis=0, tiled=True)]
    dot_general x18 -> x0, matrix products: 37 us -> none  [the longest x8 16.6 us: scores(): jnp.einsum('cd,rd->cr', candidates(block_index), query_block, preferred_e...]
    dynamic_update_slice x24 -> x0, local copies, waits for them, and re-layouts: 25.3 us -> none  [the longest x8 24.4 us: backward(): lax.dynamic_update_index_in_dim(own_grad, passage_part[:slice_rows], bloc...]
    all_to_all x4 -> x0, starting transfers between devices: 21.6 us -> none  [the longest x1 6.81 us: body(): lax.all_to_all(slot_mass.reshape(groups, CAP, slice_rows), 'dp', split_ax...]
    scatter-add x4 -> x0, other arithmetic: 20.5 us -> none  [backward(): slot_grad.at[slot_targets]]
    squeeze x12 -> x0, local copies, waits for them, and re-layouts: 16.3 us -> none  [candidates(): lax.dynamic_index_in_dim(negatives, block_index, 0, keepdims=False)]
  transfers between devices with their start and end apart: 7 -> 0, of which waited for: 4 -> 0; matrix products, arithmetic and copies ran while one was open for 7% -> 0% of each run, Pallas kernels for 0% -> 0%
where the time goes in v1:
time: 140 us
  Pallas kernels  131 us (94%)
  local copies, waits for them, and re-layouts  6.82 us (5%)
  other arithmetic  1.5 us (1%)
    pallas_call x1, Pallas kernels, reduce_call(): pl.pallas_call(kernel, out_shape=(sds((8, 128), f32), sds((per, rows, wid...  46.7 us
    pallas_call x1, Pallas kernels, body(): pl.pallas_call(gather_kernel, out_shape=(sds((inners, per, rows, width),...  44.4 us
    pallas_call x1, Pallas kernels, body(): pl.pallas_call(backward_kernel, out_shape=(sds((2, slots, half, width), b...  17.7 us
    pallas_call x1, Pallas kernels, body(): pl.pallas_call(forward_kernel, out_shape=(sds((per, cands, full_rows), f3...  11.2 us
    pallas_call x1, Pallas kernels, body(): pl.pallas_call(functools.partial(stats_kernel, groups, inners, rows), out...  11 us
    unnamed x5, local copies, waits for them, and re-layouts  4.51 us

profile of v1, /device:TPU:0, one launch (start us, length us, event | category | flops | bytes accessed | tf_op | source)
XLA Modules:
  0.0 140.0 jit_solution(8184732166623058868)
XLA Ops:
  0.6 0.6 pad_add_fusion.where
  1.2 0.8 copy.16.lists
  2.0 0.0 copy-start
  2.0 0.1 eq.43
  2.1 0.2 fusion
  2.3 0.1 copy.17
  2.3 0.1 copy.18
  2.4 0.1 multiply_reduce_fusion
  2.6 0.1 copy.22
  2.6 0.7 copy.23.table
  3.3 0.1 copy.19
  3.4 0.1 copy.20
  3.4 0.6 compare_select_fusion.1.rank
  4.1 44.4 %gather.1 = (bf16[8,4,64,1024]{3,2,1,0:T(8,128)(2,1)}, bf16[2,32,32,1024]{3,2,1,0:T(8,128)(2,1)}) custom-call(s32[16,32]{1,0:T(8,128)} %copy.23.table, bf16[4,64,1024]{2,1,0:T(8,128)(2,1)} %q_ref.1, bf16[4,64,1024]{2,1,0:T(8,128)(2,1)} %p_ref.5), custom_call_target="tpu_custom_call" | custom-call | tf_op jit(solution)/shard_map/gather/pallas_call | solution.py:567
  48.4 0.0 copy-done
  48.4 11.2 %forward.1 = (f32[4,576,512]{2,1,0:T(8,128)}, f32[4,512]{1,0:T(4,128)}, f32[32,128]{1,0:T(8,128)}, f32[8,128]{1,0:T(8,128)}) custom-call(s32[2]{0:T(128)} %pad_add_fusion.where, s32[16,64]{1,0:T(8,128)} %compare_select_fusion.1.rank, s32[64,8]{1,0:T(8,128)} %copy-done, bf16[4,64,1024]{2,1,0:T(8,128)(2,1)} %p_ref.5, ...), custom_call_target="tpu_custom_call" | custom-call | tf_op jit(solution)/shard_map/forward/pallas_call | solution.py:578
  59.6 11.0 %stats.1 = (f32[4,512]{1,0:T(4,128)}, f32[32,128]{1,0:T(8,128)}, f32[8,128]{1,0:T(8,128)}) custom-call(f32[4,512]{1,0:T(4,128)} %get-tuple-element.21.row_in, f32[32,128]{1,0:T(8,128)} %get-tuple-element.22.dense_in, f32[8,128]{1,0:T(8,128)} %get-tuple-element.23.own_in), custom_call_target="tpu_custom_call" | custom-call | tf_op jit(solution)/shard_map/stats/pallas_call | solution.py:587
  70.6 17.7 %backward.1 = (bf16[2,32,32,1024]{3,2,1,0:T(8,128)(2,1)}, bf16[8,4,64,1024]{3,2,1,0:T(8,128)(2,1)}, f32[4,64,1024]{2,1,0:T(8,128)}) custom-call(s32[2]{0:T(128)} %pad_add_fusion.where, s32[16,64]{1,0:T(8,128)} %compare_select_fusion.1.rank, s32[64,8]{1,0:T(8,128)} %copy-done, bf16[4,64,1024]{2,1,0:T(8,128)(2,1)} %p_ref.5, ...), custom_call_target="tpu_custom_call" | custom-call | tf_op jit(solution)/shard_map/backward/pallas_call | solution.py:596
  88.3 46.7 %reduce.1 = (f32[8,128]{1,0:T(8,128)}, bf16[4,64,1024]{2,1,0:T(8,128)(2,1)}, bf16[4,64,1024]{2,1,0:T(8,128)(2,1)}, f32[4,64,1024]{2,1,0:T(8,128)}) custom-call(s32[16,64]{1,0:T(8,128)} %compare_select_fusion.1.rank, bf16[2,32,32,1024]{3,2,1,0:T(8,128)(2,1)} %get-tuple-element.26.part_ref, bf16[8,4,64,1024]{3,2,1,0:T(8,128)(2,1)} %get-tuple-element.27.query_ref, ...), custom_call_target="tpu_custom_call" | custom-call | tf_op jit(solution)/shard_map/reduce/pallas_call | solution.py:624
  135.0 1.2 slice.3
  136.2 1.9 %copy.28 = bf16[4,64,1024]{2,1,0:T(8,128)(2,1)} copy(bf16[4,64,1024]{2,1,0:T(8,128)(2,1)} %get-tuple-element.37) | data formatting | bytes 1048576
  138.1 1.9 %copy.29 = bf16[4,64,1024]{2,1,0:T(8,128)(2,1)} copy(bf16[4,64,1024]{2,1,0:T(8,128)(2,1)} %get-tuple-element.38) | data formatting | bytes 1048576
  (4 shorter events, 0.0 us)
Async XLA Ops:
  2.0 46.4 %copy-start = (s32[64,8]{1,0:T(8,128)}, s32[64,8]{1,0:T(8,128)S(1)}, u32[]{:S(2)}) copy-start(s32[64,8]{1,0:T(8,128)S(1)} %copy.16.lists) | copy-start | bytes 6148

commit v2 on v0

v2 whole, which is shorter than its diff:
```python
import functools
import math

import jax
import jax.numpy as jnp
from jax import lax
from jax.experimental import pallas as pl
from jax.experimental.pallas import tpu as pltpu
from jax.sharding import PartitionSpec as P

MESH = pl.DeviceIdType.MESH
NEG = -1e30
SIDE = 4
CAP = 2
VMEM_LIMIT = 62 * 1024 * 1024

VM = pl.BlockSpec(memory_space=pltpu.VMEM)
SM = pl.BlockSpec(memory_space=pltpu.SMEM)


def mod4(v):
    return lax.rem(v + SIDE, SIDE)


class Place:
    def __init__(self):
        self.dp = lax.axis_index("dp")
        self.inner = lax.axis_index("inner")
        self.y, self.x = self.dp // SIDE, lax.rem(self.dp, SIDE)
        self.z, self.c = self.inner // 2, lax.rem(self.inner, 2)

    def move(self, axis, step):
        if axis == "x":
            return (self.y * SIDE + mod4(self.x + step), self.inner)
        if axis == "y":
            return (mod4(self.y + step) * SIDE + self.x, self.inner)
        if axis == "z":
            return (self.dp, mod4(self.z + step) * 2 + self.c)
        return (self.dp, self.z * 2 + (1 - self.c))

    def group(self, first, rf, rt):
        if first == "y":
            return mod4(self.y + rf) * SIDE + mod4(self.x + rt)
        return mod4(self.y + rt) * SIDE + mod4(self.x + rf)


class Copies:
    def __init__(self, send_sem, recv_sem):
        self.send_sem, self.recv_sem, self.count, self.made = send_sem, recv_sem, 0, []

    def send(self, src, dst, device, landing=None):
        i = self.count
        self.count += 1
        copy = pltpu.make_async_remote_copy(
            src_ref=src, dst_ref=dst, send_sem=self.send_sem.at[i], recv_sem=self.recv_sem.at[i],
            device_id=device, device_id_type=MESH)
        copy.start()
        self.made.append(copy)
        if landing is None:
            return copy
        return pltpu.make_async_remote_copy(
            src_ref=src, dst_ref=landing, send_sem=self.send_sem.at[i],
            recv_sem=self.recv_sem.at[i], device_id=device, device_id_type=MESH)

    def drain(self):
        for copy in self.made:
            copy.wait_send()


def meet(devices):
    barrier = pltpu.get_barrier_semaphore()
    for device in devices:
        pl.semaphore_signal(barrier, inc=1, device_id=device, device_id_type=MESH)
    pl.semaphore_wait(barrier, len(devices))


def neighbours(me):
    return [me.move(a, s) for a in "xyz" for s in (1, -1)] + [me.move("core", 0)]


HALVES = (("y", "x"), ("x", "y"))


def fused_kernel(dims, spec, table, rank, spot, lists, q_ref, p_ref, loss_out, qg_ref, pg_ref,
                 *scratch):
    chunks, groups, inners = dims
    me = Place()
    per, rows, width = p_ref.shape
    half, two = rows // 2, per // 2
    deep = half // chunks
    picks = lists.shape[1]
    cands = picks + 1
    queries = inners * rows
    slots = groups * CAP
    f32, b16 = jnp.float32, jnp.bfloat16
    scale = 1.0 / math.sqrt(width)
    count = 2.0 * groups * per * queries
    take = dict(zip(spec, split_list(scratch, spec.values())))
    one = lambda name: take[name][0]
    full, stage, relay, relay2 = one("full"), one("stage"), one("relay"), one("relay2")
    got, logit, weight, prod = take["got"], take["logit"], take["weight"], take["prod"]
    cand, cols, row_part = one("cand"), one("cols"), one("row_part")
    row_src, dense_src, all_rows = one("row_src"), one("dense_src"), one("all_rows")
    all_dense, row_lse, pass_lse = one("all_dense"), one("row_lse"), one("pass_lse")
    part, query_part, own_sum = one("part"), one("query_part"), one("own_sum")
    dense, merge, last = one("dense"), one("merge"), one("last")
    pair_in, qsum, zmerge, zlast = one("pair_in"), one("qsum"), one("zmerge"), one("zlast")
    loss_dp, loss_inner, loss_mid = one("loss_dp"), one("loss_inner"), one("loss_mid")
    near = [[(None,) + take["near"][(ch * 2 + h) * 3:(ch * 2 + h) * 3 + 3] for h in (0, 1)]
            for ch in range(chunks)]
    seen = [[take["seen"][(h * 3 + st) * SIDE:(h * 3 + st + 1) * SIDE] for st in range(3)]
            for h in (0, 1)]
    net = Copies(one("send_sem"), one("recv_sem"))

    dp_peers = [(lax.rem(me.dp + o, groups), me.inner) for o in range(1, groups)]
    dp_from = [lax.rem(me.dp - o + groups, groups) for o in range(1, groups)]
    in_peers = [(me.dp, lax.rem(me.inner + o, inners)) for o in range(1, inners)]
    in_from = [lax.rem(me.inner - o + inners, inners) for o in range(1, inners)]
    meet(dp_peers + in_peers)

    span = lambda h, ch: pl.ds(h * half + ch * deep, deep)
    first, second, relays, arrivals = {}, {}, {}, {ch: [] for ch in range(chunks)}

    def send_own(ch):
        for h, (f, t) in enumerate(HALVES):
            mine = p_ref.at[:, span(h, ch)]
            first[ch, h] = (net.send(mine, near[ch][h][3], me.move(f, 1)),
                            net.send(mine, near[ch][h][1], me.move(f, -1)))

    def send_second(ch):
        for h, (f, t) in enumerate(HALVES):
            up, down = first[ch, h]
            up.wait_recv()
            a = net.send(near[ch][h][3].at[0:two], near[ch][h][2].at[0:two], me.move(f, 1))
            down.wait_recv()
            b = net.send(near[ch][h][1].at[two:per], near[ch][h][2].at[two:per], me.move(f, -1))
            second[ch, h] = (a, b)

    def spread(ch, rf):
        for h, (f, t) in enumerate(HALVES):
            if rf == 2:
                for copy in second[ch, h]:
                    copy.wait_recv()
            source = me.group(f, rf, 0)
            for dt in (2, 1, 3, 0):
                if dt == 0 and rf == 0:
                    got[ch][h, 0:CAP] = jnp.zeros((CAP, deep, width), b16)
                    continue
                group = me.group(f, 0, dt)
                for c in range(CAP):
                    pick = table[group, source * CAP + c]
                    block = p_ref[pick, span(h, ch)] if rf == 0 else near[ch][h][rf][pick]
                    if dt == 0:
                        got[ch][h, rf * CAP + c] = block
                    else:
                        stage[ch, h, dt - 1, rf, c] = block
            up, down = me.move(t, 1), me.move(t, -1)
            relays[ch, h, rf] = (
                net.send(stage.at[ch, h, 1, rf, 0], relay.at[ch, h, 0, rf], up),
                net.send(stage.at[ch, h, 1, rf, 1], relay.at[ch, h, 1, rf], down))
            arrivals[ch].append(net.send(
                stage.at[ch, h, 0, rf], got[ch].at[h, pl.ds(24 + rf * CAP, CAP)], up))
            arrivals[ch].append(net.send(
                stage.at[ch, h, 2, rf], got[ch].at[h, pl.ds(8 + rf * CAP, CAP)], down))

    def pass_on(ch, *rfs):
        for rf in rfs:
            for h, (f, t) in enumerate(HALVES):
                for side, copy in enumerate(relays[ch, h, rf]):
                    copy.wait_recv()
                    arrivals[ch].append(net.send(
                        relay.at[ch, h, side, rf], got[ch].at[h, 16 + rf * CAP + side],
                        me.move(t, 1 - 2 * side)))

    at = lambda z, c: full.at[mod4(z) * 2 + c]
    own_slot = at(me.z, me.c)
    send_own(0)
    z_up = net.send(q_ref, own_slot, me.move("z", 1), at(me.z - 1, me.c))
    z_down = net.send(q_ref, own_slot, me.move("z", -1), at(me.z + 1, me.c))
    pair = [net.send(q_ref, own_slot, me.move("core", 0), at(me.z, 1 - me.c))]
    keep = pltpu.make_async_copy(q_ref, own_slot, one("local_sem"))
    keep.start()
    spread(0, 0)
    for ch in range(1, chunks):
        send_own(ch)
    send_second(0)
    spread(0, 1)
    spread(0, 3)
    z_up.wait_recv()
    behind, ahead = at(me.z - 1, me.c), at(me.z + 1, me.c)
    across = mod4(me.z + 2) * 2
    far = full.at[across + me.c]
    za = net.send(behind.at[0:two], behind.at[0:two], me.move("z", 1), far.at[0:two])
    pair.append(net.send(behind, behind, me.move("core", 0), at(me.z - 1, 1 - me.c)))
    z_down.wait_recv()
    zb = net.send(ahead.at[two:per], ahead.at[two:per], me.move("z", -1), far.at[two:per])
    pair.append(net.send(ahead, ahead, me.move("core", 0), at(me.z + 1, 1 - me.c)))
    pass_on(0, 0)
    for ch in range(1, chunks):
        send_second(ch)
    spread(0, 2)
    for ch in range(1, chunks):
        spread(ch, 0)
        pass_on(ch - 1, 1, 3)
        spread(ch, 1)
        spread(ch, 3)
        if ch == 1:
            za.wait_recv()
            zb.wait_recv()
            pair.append(
                net.send(far, far, me.move("core", 0), full.at[across + 1 - me.c]))
        pass_on(ch - 1, 2)
        spread(ch, 2)
        pass_on(ch, 0)
    if chunks == 1:
        za.wait_recv()
        zb.wait_recv()
        pair.append(net.send(far, far, me.move("core", 0), full.at[across + 1 - me.c]))

    lane = lax.broadcasted_iota(jnp.int32, (2 * deep, 128), 1)
    sub = lax.broadcasted_iota(jnp.int32, (2 * deep, 128), 0)
    wide_lane = lax.broadcasted_iota(jnp.int32, (2 * deep, queries), 1)
    wide_sub = lax.broadcasted_iota(jnp.int32, (2 * deep, queries), 0)

    def true_row(ch, sub):
        return (sub // deep) * half + ch * deep + lax.rem(sub, deep)

    def load_candidates(ch, b):
        cand[0:deep] = p_ref[b, span(0, ch)]
        cand[deep:2 * deep] = p_ref[b, span(1, ch)]
        for k in range(picks):
            block = lists[me.dp * per + b, k]
            group = block // per
            r = rank[me.dp, block]
            ry = mod4(group // SIDE - me.y)
            rx = mod4(lax.rem(group, SIDE) - me.x)
            base = 2 * deep * (k + 1)
            cand[base:base + deep] = got[ch][0, rx * 8 + ry * 2 + r]
            cand[base + deep:base + 2 * deep] = got[ch][1, ry * 8 + rx * 2 + r]

    def forward(ch, b):
        load_candidates(ch, b)
        q = full[:, b].reshape(queries, width)
        logit[ch][b] = lax.dot_general(
            cand[...], q, (((1,), (1,)), ((), ())), preferred_element_type=f32) * scale
        peak = jnp.full((1, queries), NEG, f32)
        for i in range(cands):
            block = logit[ch][b, i * 2 * deep:(i + 1) * 2 * deep]
            peak = jnp.maximum(peak, jnp.max(block, axis=0, keepdims=True))
            top = jnp.max(block, axis=1, keepdims=True)
            lse = top + jnp.log(jnp.sum(jnp.exp(block - top), axis=1, keepdims=True))
            if i == 0:
                hit = wide_lane == true_row(ch, wide_sub) + me.inner * rows
                own_sum[...] += jnp.sum(jnp.where(hit, block, 0.0))
            row = jnp.sum(jnp.where(lax.rem(lane, 64) == true_row(ch, sub), lse, 0.0), axis=0,
                          keepdims=True)
            if ch:
                row = row + cols[b, i:i + 1]
            cols[b, i:i + 1] = row
        total = jnp.zeros((1, queries), f32)
        for i in range(cands):
            block = logit[ch][b, i * 2 * deep:(i + 1) * 2 * deep]
            total = total + jnp.sum(jnp.exp(block - peak), axis=0, keepdims=True)
        row_part[ch, pl.ds(b, 1)] = peak + jnp.log(total)

    def run(fn, ch, start, stop):
        def step(b, carry):
            fn(ch, b)
            return carry

        lax.fori_loop(start, stop, step, 0)

    own_sum[...] = jnp.zeros(own_sum.shape, f32)
    for ch in range(chunks):
        last_one = ch == chunks - 1
        if last_one:
            if ch == 0:
                pass_on(ch, 1, 3)
            pass_on(ch, 2)
        for copy in arrivals[ch]:
            copy.wait_recv()
        if ch == 0:
            for copy in pair:
                copy.wait_recv()
            keep.wait()
        run(forward, ch, 0, two)
        if not last_one:
            pass_on(ch + 1, 1, 3)
        run(forward, ch, two, per)

    def fold(values):
        top = jnp.max(values, axis=0)
        return top + jnp.log(jnp.sum(jnp.exp(values - top[None]), axis=0))

    rows_mine = fold(row_part[...])
    row_src[...] = rows_mine
    stat_waits = [net.send(row_src, all_rows.at[me.inner], to, all_rows.at[origin])
                  for to, origin in zip(in_peers, in_from)]
    line = lax.broadcasted_iota(jnp.int32, (32, 128), 0)
    side = lax.broadcasted_iota(jnp.int32, (32, 128), 1) // 64
    home = line + 32 * side

    def block_of(b, i):
        return me.dp * per + b if i == 0 else lists[me.dp * per + b, i - 1]

    def raise_peak(b, peak):
        for i in range(cands):
            peak = jnp.where(home == block_of(b, i), jnp.maximum(peak, cols[b, i:i + 1]), peak)
        return peak

    peaks = lax.fori_loop(0, per, raise_peak, jnp.full((32, 128), NEG, f32))

    def add_mass(b, mass):
        for i in range(cands):
            mass = mass + jnp.where(home == block_of(b, i), jnp.exp(cols[b, i:i + 1] - peaks), 0.0)
        return mass

    mass = lax.fori_loop(0, per, add_mass, jnp.zeros((32, 128), f32))
    dense_mine = jnp.where(mass > 0.0, peaks + jnp.log(jnp.where(mass > 0.0, mass, 1.0)), NEG)
    dense_src[...] = dense_mine
    stat_waits += [net.send(dense_src, all_dense.at[me.dp], to, all_dense.at[origin])
                   for to, origin in zip(dp_peers, dp_from)]
    all_rows[me.inner] = rows_mine
    all_dense[me.dp] = dense_mine
    for copy in stat_waits:
        copy.wait_recv()
    rows_all, dense_all = fold(all_rows[...]), fold(all_dense[...])
    row_lse[...] = rows_all
    pass_lse[...] = dense_all
    where = lax.broadcasted_iota(jnp.int32, rows_all.shape, 1) // rows
    local = jnp.sum(jnp.where(where == me.inner, rows_all, 0.0))
    local = local + jnp.sum(jnp.where(home // per == me.dp, dense_all, 0.0))
    loss_mid[0] = local - 2.0 * own_sum[...]

    def weigh(ch, b):
        q = full[:, b].reshape(queries, width)
        row = row_lse[pl.ds(b, 1)]
        for i in range(cands):
            block = block_of(b, i)
            values = pass_lse[pl.ds(lax.rem(block, 32), 1)]
            pick = lane == true_row(ch, sub) + (block // 32) * 64
            col = jnp.sum(jnp.where(pick, values, 0.0), axis=1, keepdims=True)
            z = logit[ch][b, i * 2 * deep:(i + 1) * 2 * deep]
            probs = 0.5 * jnp.exp(z - row) + 0.5 * jnp.exp(z - col)
            if i == 0:
                hit = wide_lane == true_row(ch, wide_sub) + me.inner * rows
                probs = probs - jnp.where(hit, 1.0, 0.0)
            weight[ch][b, i * 2 * deep:(i + 1) * 2 * deep] = probs.astype(b16)
        out = jnp.dot(weight[ch][b], q, preferred_element_type=f32)
        prod[ch][b] = out.reshape(2 * cands, deep, width)

    send_rows, parts = {}, {(h, rf): [] for h in (0, 1) for rf in range(SIDE)}

    def emit(ch, rf):
        for h, (f, t) in enumerate(HALVES):
            def slot(i, carry, h=h, f=f):
                rt, c = i // CAP, lax.rem(i, CAP)
                owner = me.group(f, rf, rt)
                block = owner * per + table[me.dp, owner * CAP + c]
                acc = jnp.zeros((deep, width), f32)
                for b in range(per):
                    k = spot[me.dp * per + b, block]
                    live = (k >= 0).astype(f32)
                    acc = acc + prod[ch][b, 2 * (jnp.maximum(k, 0) + 1) + h] * live
                part[ch, h, rt * 8 + rf * CAP + c] = acc.astype(b16)
                return carry

            lax.fori_loop(CAP if rf == 0 else 0, SIDE * CAP, slot, 0)
            up, down = me.move(t, 1), me.move(t, -1)
            rel = pl.ds(ch * deep, deep)
            send_rows[ch, h, rf] = (
                net.send(part.at[ch, h, 16 + rf * CAP], relay2.at[ch, h, 0, rf], up),
                net.send(part.at[ch, h, 16 + rf * CAP + 1], relay2.at[ch, h, 1, rf], down))
            parts[h, rf] += [
                net.send(part.at[ch, h, pl.ds(8 + rf * CAP, CAP)], seen[h][2][rf].at[:, rel], up),
                net.send(part.at[ch, h, pl.ds(24 + rf * CAP, CAP)], seen[h][0][rf].at[:, rel],
                         down)]

    def forward_parts(ch, *rfs):
        for rf in rfs:
            for h, (f, t) in enumerate(HALVES):
                for side_, copy in enumerate(send_rows[ch, h, rf]):
                    copy.wait_recv()
                    parts[h, rf].append(net.send(
                        relay2.at[ch, h, side_, rf],
                        seen[h][1][rf].at[side_, pl.ds(ch * deep, deep)],
                        me.move(t, 1 - 2 * side_)))

    for ch in range(chunks):
        run(weigh, ch, 0, per)
        for rf in (2, 1, 3, 0):
            emit(ch, rf)

    loss_waits = [net.send(loss_mid.at[0], loss_dp.at[me.dp], to, loss_dp.at[origin])
                  for to, origin in zip(dp_peers, dp_from)]
    loss_dp[me.dp] = loss_mid[0]

    def query_grad(_, b):
        acc = None
        for ch in range(chunks):
            load_candidates(ch, b)
            grad = lax.dot_general(weight[ch][b], cand[...], (((0,), (0,)), ((), ())),
                                   preferred_element_type=f32)
            acc = grad if acc is None else acc + grad
        query_part[:, b] = acc.astype(b16).reshape(inners, rows, width)

    swaps = {}

    def swap(lo):
        for dz in (2, 1, 3, 0):
            src = query_part.at[mod4(me.z + dz) * 2 + 1 - me.c, pl.ds(lo, two)]
            swaps[dz, lo] = net.send(src, pair_in.at[dz, pl.ds(lo, two)], me.move("core", 0))

    def join(dz, lo):
        swaps[dz, lo].wait_recv()
        slot = mod4(me.z + dz) * 2 + me.c

        def step(j, carry):
            both = query_part[slot, j].astype(f32) + pair_in[dz, j].astype(f32)
            qsum[dz, j] = both.astype(b16)
            return carry

        lax.fori_loop(lo, lo + two, step, 0)

    def fold_in(target, rd, source, start):
        def step(j, carry):
            both = target[rd, start + j].astype(f32) + source[j].astype(f32)
            target[rd, start + j] = both.astype(b16)
            return carry

        lax.fori_loop(0, two, step, 0)

    run(query_grad, 0, 0, two)
    swap(0)
    forward_parts(0, 2)
    run(query_grad, 0, two, per)
    swap(two)
    forward_parts(0, 1, 3)
    join(2, 0)
    za = net.send(qsum.at[2, 0:two], zmerge.at[0], me.move("z", 1))
    join(2, two)
    zb = net.send(qsum.at[2, two:per], zmerge.at[1], me.move("z", -1))
    for lo in (0, two):
        join(1, lo)
        join(3, lo)
    forward_parts(0, 0)
    for ch in range(1, chunks):
        forward_parts(ch, 2)
    za.wait_recv()
    fold_in(qsum, 1, zmerge.at[0], 0)
    z_up = net.send(qsum.at[1], zlast.at[0], me.move("z", 1))
    zb.wait_recv()
    fold_in(qsum, 3, zmerge.at[1], two)
    z_down = net.send(qsum.at[3], zlast.at[1], me.move("z", -1))
    for copy in loss_waits:
        copy.wait_recv()
    mid = jnp.sum(loss_dp[...], axis=0)
    loss_mid[1] = mid
    loss_waits = [net.send(loss_mid.at[1], loss_inner.at[me.inner], to, loss_inner.at[origin])
                  for to, origin in zip(in_peers, in_from)]
    loss_inner[me.inner] = mid

    def collect(h, rf, j):
        f, t = HALVES[h]
        owner = me.group(f, rf, 0)
        acc = [jnp.zeros((deep, width), f32) for _ in range(chunks)]
        for st in range(SIDE):
            if st == 0 and rf == 0:
                continue
            r = rank[me.group(f, 0, st), owner * per + j]
            live = (r >= 0).astype(f32)
            c = jnp.maximum(r, 0)
            for ch in range(chunks):
                if st == 0:
                    block = part[ch, h, rf * CAP + c]
                else:
                    block = seen[h][st - 1][rf][c, ch * deep:(ch + 1) * deep]
                acc[ch] = acc[ch] + block.astype(f32) * live
        return acc

    def gather_parts(h, rf):
        for copy in parts[h, rf]:
            copy.wait_recv()

        def step(j, carry):
            for ch, acc in enumerate(collect(h, rf, j)):
                dense[h, rf - 1, j, ch * deep:(ch + 1) * deep] = acc.astype(b16)
            return carry

        lax.fori_loop(0, per, step, 0)

    merges = {}
    for ch in range(1, chunks):
        forward_parts(ch, 1, 3)
    for h, (f, t) in enumerate(HALVES):
        gather_parts(h, 2)
        merges[h] = [net.send(dense.at[h, 1, 0:two], merge.at[h, 0], me.move(f, 1)),
                     net.send(dense.at[h, 1, two:per], merge.at[h, 1], me.move(f, -1))]
    for ch in range(1, chunks):
        forward_parts(ch, 0)
    ends = []
    for h, (f, t) in enumerate(HALVES):
        for rf, slot in ((1, 0), (3, 1)):
            gather_parts(h, rf)
            merges[h][slot].wait_recv()
            fold_in(dense.at[h], rf - 1, merge.at[h, slot], slot * two)
            ends.append(net.send(dense.at[h, rf - 1], last.at[h, slot],
                                 me.move(f, 1 if slot == 0 else -1)))
    for lo in (0, two):
        swaps[0, lo].wait_recv()
    z_up.wait_recv()
    z_down.wait_recv()
    mine = me.z * 2 + me.c

    def finish_query(j, carry):
        both = query_part[mine, j].astype(f32) + pair_in[0, j].astype(f32)
        both = both + zlast[0, j].astype(f32) + zlast[1, j].astype(f32)
        qg_ref[j] = both.astype(b16)
        return carry

    lax.fori_loop(0, per, finish_query, 0)
    for copy in loss_waits:
        copy.wait_recv()
    loss_out[...] = jnp.sum(loss_inner[...], axis=0) * (1.0 / count)
    for copy in parts[0, 0] + parts[1, 0] + ends:
        copy.wait_recv()
    for h in (0, 1):
        def finish(j, carry, h=h):
            for ch, acc in enumerate(collect(h, 0, j)):
                near_rows = slice(ch * deep, (ch + 1) * deep)
                acc = acc + prod[ch][j, h]
                acc = acc + last[h, 0, j, near_rows].astype(f32)
                acc = acc + last[h, 1, j, near_rows].astype(f32)
                pg_ref[j, h * half + ch * deep:h * half + (ch + 1) * deep] = acc.astype(b16)
            return carry

        lax.fori_loop(0, per, finish, 0)
    net.drain()


def split_list(items, counts):
    out, start = [], 0
    for n in counts:
        out.append(tuple(items[start:start + n]))
        start += n
    return out


def tables(neg_lists, groups, per):
    blocks = neg_lists.shape[0]
    ids = jnp.arange(blocks, dtype=jnp.int32)
    lists = neg_lists.reshape(groups, -1)
    present = jnp.any(lists[:, :, None] == ids[None, None, :], axis=1)
    quads = present.reshape(groups, groups, per).astype(jnp.int32)
    earlier = (jnp.arange(per)[:, None] < jnp.arange(per)[None, :]).astype(jnp.int32)
    rank = jnp.sum(quads[:, :, :, None] * earlier[None, None], axis=2)
    rank = jnp.where(quads == 1, rank, -1)
    slot = jnp.arange(CAP, dtype=jnp.int32)
    local = jnp.arange(per, dtype=jnp.int32)
    block = jnp.sum(
        jnp.where(rank[..., None] == slot, local[None, None, :, None], 0), axis=2)
    order = jnp.arange(neg_lists.shape[1], dtype=jnp.int32)
    match = neg_lists[:, :, None] == ids[None, None, :]
    spot = jnp.max(jnp.where(match, order[None, :, None], -1), axis=1)
    return rank.reshape(groups, blocks), block.reshape(groups, groups * CAP), spot


CHUNKS = 1


def body(queries, passages, neg_lists):
    per, rows, width = queries.shape
    groups, inners = lax.axis_size("dp"), lax.axis_size("inner")
    picks = neg_lists.shape[1]
    half, two = rows // 2, per // 2
    slots = groups * CAP
    chunks = CHUNKS
    deep = half // chunks
    cands, full_rows = picks + 1, rows * inners
    tall = cands * 2 * deep
    b16, f32 = jnp.bfloat16, jnp.float32
    sds = jax.ShapeDtypeStruct
    rank, block, spot = tables(neg_lists, groups, per)
    v = pltpu.VMEM
    sem_count = 100 + 160 * chunks
    need = {
        "full": [v((inners, per, rows, width), b16)],
        "stage": [v((chunks, 2, SIDE - 1, SIDE, CAP, deep, width), b16)],
        "relay": [v((chunks, 2, 2, SIDE, deep, width), b16)],
        "relay2": [v((chunks, 2, 2, SIDE, deep, width), b16)],
        "got": [v((2, slots, deep, width), b16)] * chunks,
        "logit": [v((per, tall, full_rows), f32)] * chunks,
        "weight": [v((per, tall, full_rows), b16)] * chunks,
        "prod": [v((per, 2 * cands, deep, width), f32)] * chunks,
        "cand": [v((tall, width), b16)],
        "cols": [v((per, cands, 128), f32)],
        "row_part": [v((chunks, per, full_rows), f32)],
        "row_src": [v((per, full_rows), f32)],
        "dense_src": [v((32, 128), f32)],
        "all_rows": [v((inners, per, full_rows), f32)],
        "all_dense": [v((groups, 32, 128), f32)],
        "row_lse": [v((per, full_rows), f32)],
        "pass_lse": [v((32, 128), f32)],
        "part": [v((chunks, 2, slots, deep, width), b16)],
        "query_part": [v((inners, per, rows, width), b16)],
        "own_sum": [v((8, 128), f32)],
        "dense": [v((2, SIDE - 1, per, half, width), b16)],
        "merge": [v((2, 2, two, half, width), b16)],
        "last": [v((2, 2, per, half, width), b16)],
        "pair_in": [v((SIDE, per, rows, width), b16)],
        "qsum": [v((SIDE, per, rows, width), b16)],
        "zmerge": [v((2, two, rows, width), b16)],
        "zlast": [v((2, per, rows, width), b16)],
        "loss_dp": [v((groups, 8, 128), f32)],
        "loss_inner": [v((inners, 8, 128), f32)],
        "loss_mid": [v((2, 8, 128), f32)],
        "near": [v((per, deep, width), b16)] * (2 * 3 * chunks),
        "seen": [v((CAP, half, width), b16)] * (2 * 3 * SIDE),
        "send_sem": [pltpu.SemaphoreType.DMA((sem_count,))],
        "recv_sem": [pltpu.SemaphoreType.DMA((sem_count,))],
        "local_sem": [pltpu.SemaphoreType.DMA],
    }
    spec = {name: len(refs) for name, refs in need.items()}
    loss, query_grad, passage_grad = pl.pallas_call(
        functools.partial(fused_kernel, (chunks, groups, inners), spec),
        out_shape=(sds((8, 128), f32), sds((per, rows, width), b16), sds((per, rows, width), b16)),
        in_specs=[SM, SM, SM, SM, VM, VM], out_specs=(VM, VM, VM),
        scratch_shapes=[ref for refs in need.values() for ref in refs],
        compiler_params=pltpu.CompilerParams(
            vmem_limit_bytes=VMEM_LIMIT, collective_id=0, has_side_effects=True),
        name="fused",
    )(block, rank, spot, neg_lists, queries, passages)
    return (loss[0, 0], query_grad, passage_grad)


def solution(mesh):
    in_specs = (P("dp", "inner", None), P("dp", "inner", None), P())
    out_specs = (P(), P("dp", "inner", None), P("dp", "inner", None))
    return jax.shard_map(body, mesh=mesh, in_specs=in_specs, out_specs=out_specs, check_vma=False)
```

time: 456 us -> 108 us (0.24)
  blocking collectives: 135 us -> 0 us
  waiting for transfers between devices: 108 us -> 0 us
  Pallas kernels: 0 us -> 99.4 us
  local copies, waits for them, and re-layouts: 82.3 us -> 5.8 us
  matrix products: 37 us -> 0 us
  other arithmetic: 36.1 us -> 1.7 us
  starting transfers between devices: 21.9 us -> 0 us
  between operations: 17.2 us -> 0.68 us
  loops' own time: 16.1 us -> 0 us
    psum x2 -> x0, blocking collectives: 122 us -> none  [the longest x1 109 us: body(): lax.psum(local_loss, ('dp', 'inner'))]
    pallas_call x0 -> x1, Pallas kernels: none -> 99.4 us  [body(): pl.pallas_call(functools.partial(fused_kernel, (chunks, groups, inners),...]
    all_gather x2 -> x0, waiting for transfers between devices: 93.2 us -> none  [the longest x1 70.1 us: body(): shard_rows = lax.all_gather(passages, 'dp', axis=0, tiled=True)]
    dot_general x18 -> x0, matrix products: 37 us -> none  [the longest x8 16.6 us: scores(): jnp.einsum('cd,rd->cr', candidates(block_index), query_block, preferred_e...]
    dynamic_update_slice x24 -> x0, local copies, waits for them, and re-layouts: 25.3 us -> none  [the longest x8 24.4 us: backward(): lax.dynamic_update_index_in_dim(own_grad, passage_part[:slice_rows], bloc...]
    all_to_all x4 -> x0, starting transfers between devices: 21.6 us -> none  [the longest x1 6.81 us: body(): lax.all_to_all(slot_mass.reshape(groups, CAP, slice_rows), 'dp', split_ax...]
    scatter-add x4 -> x0, other arithmetic: 20.5 us -> none  [backward(): slot_grad.at[slot_targets]]
    squeeze x12 -> x0, local copies, waits for them, and re-layouts: 16.3 us -> none  [candidates(): lax.dynamic_index_in_dim(negatives, block_index, 0, keepdims=False)]
  transfers between devices with their start and end apart: 7 -> 0, of which waited for: 4 -> 0; matrix products, arithmetic and copies ran while one was open for 7% -> 0% of each run, Pallas kernels for 0% -> 0%
where the time goes in v2:
time: 108 us
  Pallas kernels  99.4 us (92%)
  local copies, waits for them, and re-layouts  5.8 us (5%)
  other arithmetic  1.7 us (2%)
    pallas_call x1, Pallas kernels, body(): pl.pallas_call(functools.partial(fused_kernel, (chunks, groups, inners),...  99.4 us
    unnamed x7, local copies, waits for them, and re-layouts  3.5 us

profile of v2, /device:TPU:0, one launch (start us, length us, event | category | flops | bytes accessed | tf_op | source)
XLA Modules:
  0.0 107.6 jit_solution(4176183087250803984)
XLA Ops:
  0.6 0.8 copy.16.lists
  1.4 0.0 copy-start
  1.4 0.1 eq.56
  1.5 0.2 fusion
  1.7 0.1 copy.17
  1.7 0.1 copy.18
  1.8 0.1 multiply_reduce_fusion
  2.0 0.1 copy.20
  2.0 0.7 copy.24.table
  2.7 0.1 copy.21
  2.8 0.1 copy.22
  2.8 0.6 compare_select_fusion.1.rank
  3.5 0.0 copy-done
  3.5 0.8 select_reduce_fusion.spot
  4.3 99.4 %fused.1 = (f32[8,128]{1,0:T(8,128)}, bf16[4,64,1024]{2,1,0:T(8,128)(2,1)}, bf16[4,64,1024]{2,1,0:T(8,128)(2,1)}) custom-call(s32[16,32]{1,0:T(8,128)} %copy.24.table, s32[16,64]{1,0:T(8,128)} %compare_select_fusion.1.rank, s32[64,64]{1,0:T(8,128)} %select_reduce_fusion.spot, s32[64,8]{1,0:T(8,128)} %copy-done, bf16[4,64,1024]{2,1,0:T(8,128)(2,1)} %q_ref.1, ...), custom_call_target="tpu_custom_call" | custom-call | tf_op jit(solution)/shard_map/fused/pallas_call | solution.py:624
  103.7 1.2 %slice.3 = f32[1,1]{1,0:T(1,128)} slice(f32[8,128]{1,0:T(8,128)} %get-tuple-element.6), slice={[0:1], [0:1]} | slice | bytes 8 | tf_op jit(solution)/shard_map/slice | solution.py:633
  104.9 0.0 copy-start.1
  104.9 1.9 %copy.28 = bf16[4,64,1024]{2,1,0:T(8,128)(2,1)} copy(bf16[4,64,1024]{2,1,0:T(8,128)(2,1)} %get-tuple-element.13) | data formatting | bytes 1048576
  106.8 0.0 copy-done.1
  106.8 0.8 copy.29
  (4 shorter events, 0.0 us)
Async XLA Ops:
  1.4 2.0 %copy-start = (s32[64,8]{1,0:T(8,128)}, s32[64,8]{1,0:T(8,128)S(1)}, u32[]{:S(2)}) copy-start(s32[64,8]{1,0:T(8,128)S(1)} %copy.16.lists) | copy-start | bytes 6148
  104.9 1.9 %copy-start.1 = (bf16[4,64,1024]{2,1,0:T(8,128)(2,1)S(1)}, bf16[4,64,1024]{2,1,0:T(8,128)(2,1)}, u32[]{:S(2)}) copy-start(bf16[4,64,1024]{2,1,0:T(8,128)(2,1)} %get-tuple-element.14) | copy-start | bytes 1572868

commit v3 on v2

--- a/solution.py
+++ b/solution.py
@@ -16,6 +16,7 @@
 
 VM = pl.BlockSpec(memory_space=pltpu.VMEM)
 SM = pl.BlockSpec(memory_space=pltpu.SMEM)
+AN = pl.BlockSpec(memory_space=pl.ANY)
 
 
 def mod4(v):
@@ -67,13 +68,6 @@
             copy.wait_send()
 
 
-def meet(devices):
-    barrier = pltpu.get_barrier_semaphore()
-    for device in devices:
-        pl.semaphore_signal(barrier, inc=1, device_id=device, device_id_type=MESH)
-    pl.semaphore_wait(barrier, len(devices))
-
-
 def neighbours(me):
     return [me.move(a, s) for a in "xyz" for s in (1, -1)] + [me.move("core", 0)]
 
@@ -81,14 +75,13 @@
 HALVES = (("y", "x"), ("x", "y"))
 
 
-def fused_kernel(dims, spec, table, rank, spot, lists, q_ref, p_ref, loss_out, qg_ref, pg_ref,
-                 *scratch):
+def fused_kernel(dims, spec, list_ref, q_hbm, p_hbm, loss_out, qg_hbm, pg_hbm, *scratch):
     chunks, groups, inners = dims
     me = Place()
-    per, rows, width = p_ref.shape
+    per, rows, width = p_hbm.shape
     half, two = rows // 2, per // 2
     deep = half // chunks
-    picks = lists.shape[1]
+    picks = list_ref.shape[1]
     cands = picks + 1
     queries = inners * rows
     slots = groups * CAP
@@ -116,7 +109,58 @@
     dp_from = [lax.rem(me.dp - o + groups, groups) for o in range(1, groups)]
     in_peers = [(me.dp, lax.rem(me.inner + o, inners)) for o in range(1, inners)]
     in_from = [lax.rem(me.inner - o + inners, inners) for o in range(1, inners)]
-    meet(dp_peers + in_peers)
+    p_ref, qg_ref, pg_ref = one("p_own"), one("qg"), one("pg")
+    local = one("local_sem")
+    mine = me.z * 2 + me.c
+    own_slot = full.at[mine]
+    load_q = pltpu.make_async_copy(q_hbm, own_slot, local.at[0])
+    load_p = pltpu.make_async_copy(p_hbm, p_ref, local.at[1])
+    load_q.start()
+    load_p.start()
+    barrier = pltpu.get_barrier_semaphore()
+    near_devices = neighbours(me)
+    for device in near_devices:
+        pl.semaphore_signal(barrier, inc=1, device_id=device, device_id_type=MESH)
+
+    tab_v, tab_s, spot_v, spot_s = one("tab_v"), one("tab_s"), one("spot_v"), one("spot_s")
+    every = list_ref[...]
+    blocks = every.shape[0]
+    lanes = lax.broadcasted_iota(jnp.int32, (blocks, 128), 1)
+    spots = jnp.full((blocks, 128), -1, jnp.int32)
+    for k in range(picks):
+        entry = every[:, k:k + 1]
+        spots = jnp.where(entry == lanes, k, spots)
+        spots = jnp.where(lanes == blocks + k, entry, spots)
+    spots = spots.reshape(groups, per, 128)
+    present = jnp.max(jnp.where(spots >= 0, 1, 0), axis=1)
+    quad = lax.rem(lax.broadcasted_iota(jnp.int32, (groups, 128), 1), per)
+    earlier = jnp.zeros((groups, 128), jnp.int32)
+    for j in range(1, per):
+        earlier = earlier + jnp.where(quad >= j, pltpu.roll(present, j, 1), 0)
+    ranks = jnp.where(present == 1, earlier, -1)
+    tab_v[0] = ranks
+    for c in range(CAP):
+        first_of = jnp.zeros((groups, 128), jnp.int32)
+        for j in range(1, per):
+            first_of = first_of + jnp.where(pltpu.roll(ranks, 128 - j, 1) == c, j, 0)
+        tab_v[1 + c] = first_of
+    spot_v[...] = spots
+    tab_copy = pltpu.make_async_copy(tab_v, tab_s, local.at[2])
+    spot_copy = pltpu.make_async_copy(spot_v.at[me.dp], spot_s, local.at[3])
+    tab_copy.start()
+    spot_copy.start()
+
+    def rank_of(group, block):
+        return tab_s[0, group, block]
+
+    def pick_of(group, source, c):
+        return tab_s[1 + c, group, source * per]
+
+    def listed(b, k):
+        return spot_s[b, blocks + k]
+
+    pl.semaphore_wait(barrier, len(near_devices))
+    load_p.wait()
 
     span = lambda h, ch: pl.ds(h * half + ch * deep, deep)
     first, second, relays, arrivals = {}, {}, {}, {ch: [] for ch in range(chunks)}
@@ -148,7 +192,7 @@
                     continue
                 group = me.group(f, 0, dt)
                 for c in range(CAP):
-                    pick = table[group, source * CAP + c]
+                    pick = pick_of(group, source, c)
                     block = p_ref[pick, span(h, ch)] if rf == 0 else near[ch][h][rf][pick]
                     if dt == 0:
                         got[ch][h, rf * CAP + c] = block
@@ -173,13 +217,13 @@
                         me.move(t, 1 - 2 * side)))
 
     at = lambda z, c: full.at[mod4(z) * 2 + c]
-    own_slot = at(me.z, me.c)
     send_own(0)
-    z_up = net.send(q_ref, own_slot, me.move("z", 1), at(me.z - 1, me.c))
-    z_down = net.send(q_ref, own_slot, me.move("z", -1), at(me.z + 1, me.c))
-    pair = [net.send(q_ref, own_slot, me.move("core", 0), at(me.z, 1 - me.c))]
-    keep = pltpu.make_async_copy(q_ref, own_slot, one("local_sem"))
-    keep.start()
+    load_q.wait()
+    z_up = net.send(own_slot, own_slot, me.move("z", 1), at(me.z - 1, me.c))
+    z_down = net.send(own_slot, own_slot, me.move("z", -1), at(me.z + 1, me.c))
+    pair = [net.send(own_slot, own_slot, me.move("core", 0), at(me.z, 1 - me.c))]
+    tab_copy.wait()
+    spot_copy.wait()
     spread(0, 0)
     for ch in range(1, chunks):
         send_own(ch)
@@ -229,9 +273,9 @@
         cand[0:deep] = p_ref[b, span(0, ch)]
         cand[deep:2 * deep] = p_ref[b, span(1, ch)]
         for k in range(picks):
-            block = lists[me.dp * per + b, k]
+            block = listed(b, k)
             group = block // per
-            r = rank[me.dp, block]
+            r = rank_of(me.dp, block)
             ry = mod4(group // SIDE - me.y)
             rx = mod4(lax.rem(group, SIDE) - me.x)
             base = 2 * deep * (k + 1)
@@ -282,7 +326,6 @@
         if ch == 0:
             for copy in pair:
                 copy.wait_recv()
-            keep.wait()
         run(forward, ch, 0, two)
         if not last_one:
             pass_on(ch + 1, 1, 3)
@@ -301,7 +344,7 @@
     home = line + 32 * side
 
     def block_of(b, i):
-        return me.dp * per + b if i == 0 else lists[me.dp * per + b, i - 1]
+        return me.dp * per + b if i == 0 else listed(b, i - 1)
 
     def raise_peak(b, peak):
         for i in range(cands):
@@ -328,9 +371,9 @@
     row_lse[...] = rows_all
     pass_lse[...] = dense_all
     where = lax.broadcasted_iota(jnp.int32, rows_all.shape, 1) // rows
-    local = jnp.sum(jnp.where(where == me.inner, rows_all, 0.0))
-    local = local + jnp.sum(jnp.where(home // per == me.dp, dense_all, 0.0))
-    loss_mid[0] = local - 2.0 * own_sum[...]
+    loss_own = jnp.sum(jnp.where(where == me.inner, rows_all, 0.0))
+    loss_own = loss_own + jnp.sum(jnp.where(home // per == me.dp, dense_all, 0.0))
+    loss_mid[0] = loss_own - 2.0 * own_sum[...]
 
     def weigh(ch, b):
         q = full[:, b].reshape(queries, width)
@@ -356,10 +399,11 @@
             def slot(i, carry, h=h, f=f):
                 rt, c = i // CAP, lax.rem(i, CAP)
                 owner = me.group(f, rf, rt)
-                block = owner * per + table[me.dp, owner * CAP + c]
+                block = owner * per + jnp.where(
+                    c == 0, pick_of(me.dp, owner, 0), pick_of(me.dp, owner, 1))
                 acc = jnp.zeros((deep, width), f32)
                 for b in range(per):
-                    k = spot[me.dp * per + b, block]
+                    k = spot_s[b, block]
                     live = (k >= 0).astype(f32)
                     acc = acc + prod[ch][b, 2 * (jnp.maximum(k, 0) + 1) + h] * live
                 part[ch, h, rt * 8 + rf * CAP + c] = acc.astype(b16)
@@ -467,7 +511,7 @@
         for st in range(SIDE):
             if st == 0 and rf == 0:
                 continue
-            r = rank[me.group(f, 0, st), owner * per + j]
+            r = rank_of(me.group(f, 0, st), owner * per + j)
             live = (r >= 0).astype(f32)
             c = jnp.maximum(r, 0)
             for ch in range(chunks):
@@ -510,8 +554,6 @@
         swaps[0, lo].wait_recv()
     z_up.wait_recv()
     z_down.wait_recv()
-    mine = me.z * 2 + me.c
-
     def finish_query(j, carry):
         both = query_part[mine, j].astype(f32) + pair_in[0, j].astype(f32)
         both = both + zlast[0, j].astype(f32) + zlast[1, j].astype(f32)
@@ -519,6 +561,8 @@
         return carry
 
     lax.fori_loop(0, per, finish_query, 0)
+    store_q = pltpu.make_async_copy(qg_ref, qg_hbm, local.at[0])
+    store_q.start()
     for copy in loss_waits:
         copy.wait_recv()
     loss_out[...] = jnp.sum(loss_inner[...], axis=0) * (1.0 / count)
@@ -535,7 +579,11 @@
             return carry
 
         lax.fori_loop(0, per, finish, 0)
+    store_p = pltpu.make_async_copy(pg_ref, pg_hbm, local.at[1])
+    store_p.start()
     net.drain()
+    store_q.wait()
+    store_p.wait()
 
 
 def split_list(items, counts):
@@ -546,23 +594,19 @@
     return out
 
 
-def tables(neg_lists, groups, per):
-    blocks = neg_lists.shape[0]
-    ids = jnp.arange(blocks, dtype=jnp.int32)
-    lists = neg_lists.reshape(groups, -1)
-    present = jnp.any(lists[:, :, None] == ids[None, None, :], axis=1)
-    quads = present.reshape(groups, groups, per).astype(jnp.int32)
-    earlier = (jnp.arange(per)[:, None] < jnp.arange(per)[None, :]).astype(jnp.int32)
-    rank = jnp.sum(quads[:, :, :, None] * earlier[None, None], axis=2)
-    rank = jnp.where(quads == 1, rank, -1)
-    slot = jnp.arange(CAP, dtype=jnp.int32)
-    local = jnp.arange(per, dtype=jnp.int32)
-    block = jnp.sum(
-        jnp.where(rank[..., None] == slot, local[None, None, :, None], 0), axis=2)
-    order = jnp.arange(neg_lists.shape[1], dtype=jnp.int32)
-    match = neg_lists[:, :, None] == ids[None, None, :]
-    spot = jnp.max(jnp.where(match, order[None, :, None], -1), axis=1)
-    return rank.reshape(groups, blocks), block.reshape(groups, groups * CAP), spot
+def finish_kernel(loss_ref, q_ref, p_ref, loss_out, q_out, p_out, q_buf, p_buf, sem):
+    loads = [pltpu.make_async_copy(a, b, sem.at[i])
+             for i, (a, b) in enumerate(((q_ref, q_buf), (p_ref, p_buf)))]
+    stores = [pltpu.make_async_copy(b, a, sem.at[2 + i])
+              for i, (a, b) in enumerate(((q_out, q_buf), (p_out, p_buf)))]
+    for copy in loads:
+        copy.start()
+    loss_out[0, 0] = loss_ref[0, 0]
+    for copy, after in zip(loads, stores):
+        copy.wait()
+        after.start()
+    for copy in stores:
+        copy.wait()
 
 
 CHUNKS = 1
@@ -580,7 +624,6 @@
     tall = cands * 2 * deep
     b16, f32 = jnp.bfloat16, jnp.float32
     sds = jax.ShapeDtypeStruct
-    rank, block, spot = tables(neg_lists, groups, per)
     v = pltpu.VMEM
     sem_count = 100 + 160 * chunks
     need = {
@@ -618,19 +661,34 @@
         "seen": [v((CAP, half, width), b16)] * (2 * 3 * SIDE),
         "send_sem": [pltpu.SemaphoreType.DMA((sem_count,))],
         "recv_sem": [pltpu.SemaphoreType.DMA((sem_count,))],
-        "local_sem": [pltpu.SemaphoreType.DMA],
+        "local_sem": [pltpu.SemaphoreType.DMA((4,))],
+        "p_own": [v((per, rows, width), b16)],
+        "qg": [v((per, rows, width), b16)],
+        "pg": [v((per, rows, width), b16)],
+        "tab_v": [v((1 + CAP, groups, 128), jnp.int32)],
+        "tab_s": [pltpu.SMEM((1 + CAP, groups, 128), jnp.int32)],
+        "spot_v": [v((groups, per, 128), jnp.int32)],
+        "spot_s": [pltpu.SMEM((per, 128), jnp.int32)],
     }
     spec = {name: len(refs) for name, refs in need.items()}
     loss, query_grad, passage_grad = pl.pallas_call(
         functools.partial(fused_kernel, (chunks, groups, inners), spec),
         out_shape=(sds((8, 128), f32), sds((per, rows, width), b16), sds((per, rows, width), b16)),
-        in_specs=[SM, SM, SM, SM, VM, VM], out_specs=(VM, VM, VM),
+        in_specs=[VM, AN, AN], out_specs=(VM, AN, AN),
         scratch_shapes=[ref for refs in need.values() for ref in refs],
         compiler_params=pltpu.CompilerParams(
             vmem_limit_bytes=VMEM_LIMIT, collective_id=0, has_side_effects=True),
         name="fused",
-    )(block, rank, spot, neg_lists, queries, passages)
-    return (loss[0, 0], query_grad, passage_grad)
+    )(neg_lists, queries, passages)
+    shape = (per, rows, width)
+    loss, query_grad, passage_grad = pl.pallas_call(
+        finish_kernel,
+        out_shape=(sds((1, 1), f32), sds(shape, b16), sds(shape, b16)),
+        in_specs=[SM, AN, AN], out_specs=(SM, AN, AN),
+        scratch_shapes=[v(shape, b16), v(shape, b16), pltpu.SemaphoreType.DMA((4,))],
+        name="finish",
+    )(loss, query_grad, passage_grad)
+    return (loss.reshape(()), query_grad, passage_grad)
 
 
 def solution(mesh):

time: 108 us -> 103 us (0.954)
  local copies, waits for them, and re-layouts: 5.8 us -> 1.38 us
  other arithmetic: 1.7 us -> 0 us
  Pallas kernels: 99.4 us -> 101 us
    pallas_call x0 -> x1, Pallas kernels: none -> 3.28 us  [body(): pl.pallas_call(finish_kernel, out_shape=(sds((1, 1), f32), sds(shape, b16...]
    unnamed x7 -> x1, local copies, waits for them, and re-layouts: 3.5 us -> 1.38 us
    pallas_call x1, Pallas kernels: 99.4 us -> 97.7 us  [body(): pl.pallas_call(functools.partial(fused_kernel, (chunks, groups, inners),...]
    slice x1 -> x0, local copies, waits for them, and re-layouts: 1.18 us -> none  [body(): return (loss[0, 0], query_grad, passage_grad)]
where the time goes in v3:
time: 103 us
  Pallas kernels  101 us (98%)
  local copies, waits for them, and re-layouts  1.38 us (1%)
    pallas_call x1, Pallas kernels, body(): pl.pallas_call(functools.partial(fused_kernel, (chunks, groups, inners),...  97.7 us
    pallas_call x1, Pallas kernels, body(): pl.pallas_call(finish_kernel, out_shape=(sds((1, 1), f32), sds(shape, b16...  3.28 us

profile of v3, /device:TPU:0, one launch (start us, length us, event | category | flops | bytes accessed | tf_op | source)
XLA Modules:
  0.0 103.0 jit_solution(5929642841830290312)
XLA Ops:
  0.6 1.4 %copy.6.list_ref = s32[64,8]{1,0:T(8,128)} copy(s32[64,8]{0,1:T(8,128)} %param.5) | data formatting | bytes 4096 | tf_op args[2]
  2.0 97.7 %fused.1 = (f32[8,128]{1,0:T(8,128)}, bf16[4,64,1024]{2,1,0:T(8,128)(2,1)}, bf16[4,64,1024]{2,1,0:T(8,128)(2,1)}) custom-call(s32[64,8]{1,0:T(8,128)} %copy.6.list_ref, bf16[4,64,1024]{2,1,0:T(8,128)(2,1)} %q_hbm.1, bf16[4,64,1024]{2,1,0:T(8,128)(2,1)} %p_hbm.1), custom_call_target="tpu_custom_call" | custom-call | tf_op jit(solution)/shard_map/fused/pallas_call | solution.py:674
  99.7 3.3 %finish.1 = (f32[1,1]{1,0:T(1,128)}, bf16[4,64,1024]{2,1,0:T(8,128)(2,1)}, bf16[4,64,1024]{2,1,0:T(8,128)(2,1)}) custom-call(f32[8,128]{1,0:T(8,128)} %get-tuple-element.9.loss_ref, bf16[4,64,1024]{2,1,0:T(8,128)(2,1)} %get-tuple-element.10.q_ref, bf16[4,64,1024]{2,1,0:T(8,128)(2,1)} %get-tuple-element.11.p_ref), custom_call_target="tpu_custom_call" | custom-call | tf_op jit(solution)/shard_map/finish/pallas_call | solution.py:684

commit v4 on v3

--- a/solution.py
+++ b/solution.py
@@ -81,7 +81,7 @@
     per, rows, width = p_hbm.shape
     half, two = rows // 2, per // 2
     deep = half // chunks
-    picks = list_ref.shape[1]
+    picks = list_ref.shape[0]
     cands = picks + 1
     queries = inners * rows
     slots = groups * CAP
@@ -92,7 +92,7 @@
     one = lambda name: take[name][0]
     full, stage, relay, relay2 = one("full"), one("stage"), one("relay"), one("relay2")
     got, logit, weight, prod = take["got"], take["logit"], take["weight"], take["prod"]
-    cand, cols, row_part = one("cand"), one("cols"), one("row_part")
+    cand, cols, row_part = take["cand"], one("cols"), one("row_part")
     row_src, dense_src, all_rows = one("row_src"), one("dense_src"), one("all_rows")
     all_dense, row_lse, pass_lse = one("all_dense"), one("row_lse"), one("pass_lse")
     part, query_part, own_sum = one("part"), one("query_part"), one("own_sum")
@@ -123,8 +123,9 @@
         pl.semaphore_signal(barrier, inc=1, device_id=device, device_id_type=MESH)
 
     tab_v, tab_s, spot_v, spot_s = one("tab_v"), one("tab_s"), one("spot_v"), one("spot_s")
-    every = list_ref[...]
-    blocks = every.shape[0]
+    blocks = list_ref.shape[1]
+    every = jnp.transpose(jnp.concatenate(
+        [list_ref[...], jnp.zeros((picks, 128 - blocks), jnp.int32)], axis=1))[0:blocks]
     lanes = lax.broadcasted_iota(jnp.int32, (blocks, 128), 1)
     spots = jnp.full((blocks, 128), -1, jnp.int32)
     for k in range(picks):
@@ -269,67 +270,54 @@
     def true_row(ch, sub):
         return (sub // deep) * half + ch * deep + lax.rem(sub, deep)
 
-    def load_candidates(ch, b):
-        cand[0:deep] = p_ref[b, span(0, ch)]
-        cand[deep:2 * deep] = p_ref[b, span(1, ch)]
+    def load_candidates(b):
+        to = cand[b % 2]
+        to[0:half] = p_ref[b, 0:half]
+        to[half:rows] = p_ref[b, half:rows]
         for k in range(picks):
             block = listed(b, k)
             group = block // per
             r = rank_of(me.dp, block)
             ry = mod4(group // SIDE - me.y)
             rx = mod4(lax.rem(group, SIDE) - me.x)
-            base = 2 * deep * (k + 1)
-            cand[base:base + deep] = got[ch][0, rx * 8 + ry * 2 + r]
-            cand[base + deep:base + 2 * deep] = got[ch][1, ry * 8 + rx * 2 + r]
-
-    def forward(ch, b):
-        load_candidates(ch, b)
+            base = rows * (k + 1)
+            to[base:base + half] = got[0][0, rx * 8 + ry * 2 + r]
+            to[base + half:base + rows] = got[0][1, ry * 8 + rx * 2 + r]
+
+    def score(b):
+        load_candidates(b)
         q = full[:, b].reshape(queries, width)
-        logit[ch][b] = lax.dot_general(
-            cand[...], q, (((1,), (1,)), ((), ())), preferred_element_type=f32) * scale
+        logit[b][...] = lax.dot_general(
+            cand[b % 2][...], q, (((1,), (1,)), ((), ())), preferred_element_type=f32) * scale
+
+    def summarise(b):
         peak = jnp.full((1, queries), NEG, f32)
         for i in range(cands):
-            block = logit[ch][b, i * 2 * deep:(i + 1) * 2 * deep]
+            block = logit[b][i * rows:(i + 1) * rows]
             peak = jnp.maximum(peak, jnp.max(block, axis=0, keepdims=True))
             top = jnp.max(block, axis=1, keepdims=True)
             lse = top + jnp.log(jnp.sum(jnp.exp(block - top), axis=1, keepdims=True))
             if i == 0:
-                hit = wide_lane == true_row(ch, wide_sub) + me.inner * rows
+                hit = wide_lane == wide_sub + me.inner * rows
                 own_sum[...] += jnp.sum(jnp.where(hit, block, 0.0))
-            row = jnp.sum(jnp.where(lax.rem(lane, 64) == true_row(ch, sub), lse, 0.0), axis=0,
-                          keepdims=True)
-            if ch:
-                row = row + cols[b, i:i + 1]
-            cols[b, i:i + 1] = row
+            cols[b, i:i + 1] = jnp.sum(jnp.where(lax.rem(lane, 64) == sub, lse, 0.0), axis=0,
+                                       keepdims=True)
         total = jnp.zeros((1, queries), f32)
         for i in range(cands):
-            block = logit[ch][b, i * 2 * deep:(i + 1) * 2 * deep]
+            block = logit[b][i * rows:(i + 1) * rows]
             total = total + jnp.sum(jnp.exp(block - peak), axis=0, keepdims=True)
-        row_part[ch, pl.ds(b, 1)] = peak + jnp.log(total)
-
-    def run(fn, ch, start, stop):
-        def step(b, carry):
-            fn(ch, b)
-            return carry
-
-        lax.fori_loop(start, stop, step, 0)
+        row_part[0, b:b + 1] = peak + jnp.log(total)
 
     own_sum[...] = jnp.zeros(own_sum.shape, f32)
-    for ch in range(chunks):
-        last_one = ch == chunks - 1
-        if last_one:
-            if ch == 0:
-                pass_on(ch, 1, 3)
-            pass_on(ch, 2)
-        for copy in arrivals[ch]:
-            copy.wait_recv()
-        if ch == 0:
-            for copy in pair:
-                copy.wait_recv()
-        run(forward, ch, 0, two)
-        if not last_one:
-            pass_on(ch + 1, 1, 3)
-        run(forward, ch, two, per)
+    pass_on(0, 1, 3)
+    pass_on(0, 2)
+    for copy in arrivals[0] + pair:
+        copy.wait_recv()
+    score(0)
+    for b in range(1, per):
+        score(b)
+        summarise(b - 1)
+    summarise(per - 1)
 
     def fold(values):
         top = jnp.max(values, axis=0)
@@ -375,22 +363,24 @@
     loss_own = loss_own + jnp.sum(jnp.where(home // per == me.dp, dense_all, 0.0))
     loss_mid[0] = loss_own - 2.0 * own_sum[...]
 
-    def weigh(ch, b):
-        q = full[:, b].reshape(queries, width)
-        row = row_lse[pl.ds(b, 1)]
+    def weigh(b):
+        row = row_lse[b:b + 1]
         for i in range(cands):
             block = block_of(b, i)
             values = pass_lse[pl.ds(lax.rem(block, 32), 1)]
-            pick = lane == true_row(ch, sub) + (block // 32) * 64
+            pick = lane == sub + (block // 32) * 64
             col = jnp.sum(jnp.where(pick, values, 0.0), axis=1, keepdims=True)
-            z = logit[ch][b, i * 2 * deep:(i + 1) * 2 * deep]
+            z = logit[b][i * rows:(i + 1) * rows]
             probs = 0.5 * jnp.exp(z - row) + 0.5 * jnp.exp(z - col)
             if i == 0:
-                hit = wide_lane == true_row(ch, wide_sub) + me.inner * rows
+                hit = wide_lane == wide_sub + me.inner * rows
                 probs = probs - jnp.where(hit, 1.0, 0.0)
-            weight[ch][b, i * 2 * deep:(i + 1) * 2 * deep] = probs.astype(b16)
-        out = jnp.dot(weight[ch][b], q, preferred_element_type=f32)
-        prod[ch][b] = out.reshape(2 * cands, deep, width)
+            weight[b][i * rows:(i + 1) * rows] = probs.astype(b16)
+
+    def multiply(b):
+        q = full[:, b].reshape(queries, width)
+        out = jnp.dot(weight[b][...], q, preferred_element_type=f32)
+        prod[b][...] = out.reshape(2 * cands, deep, width)
 
     send_rows, parts = {}, {(h, rf): [] for h in (0, 1) for rf in range(SIDE)}
 
@@ -405,7 +395,7 @@
                 for b in range(per):
                     k = spot_s[b, block]
                     live = (k >= 0).astype(f32)
-                    acc = acc + prod[ch][b, 2 * (jnp.maximum(k, 0) + 1) + h] * live
+                    acc = acc + prod[b][2 * (jnp.maximum(k, 0) + 1) + h] * live
                 part[ch, h, rt * 8 + rf * CAP + c] = acc.astype(b16)
                 return carry
 
@@ -430,23 +420,11 @@
                         seen[h][1][rf].at[side_, pl.ds(ch * deep, deep)],
                         me.move(t, 1 - 2 * side_)))
 
-    for ch in range(chunks):
-        run(weigh, ch, 0, per)
-        for rf in (2, 1, 3, 0):
-            emit(ch, rf)
-
-    loss_waits = [net.send(loss_mid.at[0], loss_dp.at[me.dp], to, loss_dp.at[origin])
-                  for to, origin in zip(dp_peers, dp_from)]
-    loss_dp[me.dp] = loss_mid[0]
-
-    def query_grad(_, b):
-        acc = None
-        for ch in range(chunks):
-            load_candidates(ch, b)
-            grad = lax.dot_general(weight[ch][b], cand[...], (((0,), (0,)), ((), ())),
-                                   preferred_element_type=f32)
-            acc = grad if acc is None else acc + grad
-        query_part[:, b] = acc.astype(b16).reshape(inners, rows, width)
+    def query_grad(b):
+        load_candidates(b)
+        grad = lax.dot_general(weight[b][...], cand[b % 2][...], (((0,), (0,)), ((), ())),
+                               preferred_element_type=f32)
+        query_part[:, b] = grad.astype(b16).reshape(inners, rows, width)
 
     swaps = {}
 
@@ -473,36 +451,6 @@
             return carry
 
         lax.fori_loop(0, two, step, 0)
-
-    run(query_grad, 0, 0, two)
-    swap(0)
-    forward_parts(0, 2)
-    run(query_grad, 0, two, per)
-    swap(two)
-    forward_parts(0, 1, 3)
-    join(2, 0)
-    za = net.send(qsum.at[2, 0:two], zmerge.at[0], me.move("z", 1))
-    join(2, two)
-    zb = net.send(qsum.at[2, two:per], zmerge.at[1], me.move("z", -1))
-    for lo in (0, two):
-        join(1, lo)
-        join(3, lo)
-    forward_parts(0, 0)
-    for ch in range(1, chunks):
-        forward_parts(ch, 2)
-    za.wait_recv()
-    fold_in(qsum, 1, zmerge.at[0], 0)
-    z_up = net.send(qsum.at[1], zlast.at[0], me.move("z", 1))
-    zb.wait_recv()
-    fold_in(qsum, 3, zmerge.at[1], two)
-    z_down = net.send(qsum.at[3], zlast.at[1], me.move("z", -1))
-    for copy in loss_waits:
-        copy.wait_recv()
-    mid = jnp.sum(loss_dp[...], axis=0)
-    loss_mid[1] = mid
-    loss_waits = [net.send(loss_mid.at[1], loss_inner.at[me.inner], to, loss_inner.at[origin])
-                  for to, origin in zip(in_peers, in_from)]
-    loss_inner[me.inner] = mid
 
     def collect(h, rf, j):
         f, t = HALVES[h]
@@ -533,23 +481,60 @@
 
         lax.fori_loop(0, per, step, 0)
 
-    merges = {}
-    for ch in range(1, chunks):
-        forward_parts(ch, 1, 3)
+    merges, ends = {}, []
+    weigh(0)
+    for b in range(1, per):
+        multiply(b - 1)
+        weigh(b)
+    multiply(per - 1)
+    emit(0, 2)
+    emit(0, 1)
+    loss_waits = [net.send(loss_mid.at[0], loss_dp.at[me.dp], to, loss_dp.at[origin])
+                  for to, origin in zip(dp_peers, dp_from)]
+    loss_dp[me.dp] = loss_mid[0]
+    for b in range(0, two):
+        query_grad(b)
+    swap(0)
+    forward_parts(0, 2)
+    emit(0, 3)
+    for b in range(two, per):
+        query_grad(b)
+    swap(two)
+    forward_parts(0, 1)
+    join(2, 0)
+    za = net.send(qsum.at[2, 0:two], zmerge.at[0], me.move("z", 1))
+    join(2, two)
+    zb = net.send(qsum.at[2, two:per], zmerge.at[1], me.move("z", -1))
+    forward_parts(0, 3)
     for h, (f, t) in enumerate(HALVES):
         gather_parts(h, 2)
         merges[h] = [net.send(dense.at[h, 1, 0:two], merge.at[h, 0], me.move(f, 1)),
                      net.send(dense.at[h, 1, two:per], merge.at[h, 1], me.move(f, -1))]
-    for ch in range(1, chunks):
-        forward_parts(ch, 0)
-    ends = []
-    for h, (f, t) in enumerate(HALVES):
-        for rf, slot in ((1, 0), (3, 1)):
+    emit(0, 0)
+    for lo in (0, two):
+        join(1, lo)
+        join(3, lo)
+    za.wait_recv()
+    fold_in(qsum, 1, zmerge.at[0], 0)
+    z_up = net.send(qsum.at[1], zlast.at[0], me.move("z", 1))
+    zb.wait_recv()
+    fold_in(qsum, 3, zmerge.at[1], two)
+    z_down = net.send(qsum.at[3], zlast.at[1], me.move("z", -1))
+    for rf, slot in ((1, 0), (3, 1)):
+        for h, (f, t) in enumerate(HALVES):
             gather_parts(h, rf)
             merges[h][slot].wait_recv()
             fold_in(dense.at[h], rf - 1, merge.at[h, slot], slot * two)
             ends.append(net.send(dense.at[h, rf - 1], last.at[h, slot],
                                  me.move(f, 1 if slot == 0 else -1)))
+    forward_parts(0, 0)
+    for copy in loss_waits:
+        copy.wait_recv()
+    mid = jnp.sum(loss_dp[...], axis=0)
+    loss_mid[1] = mid
+    loss_waits = [net.send(loss_mid.at[1], loss_inner.at[me.inner], to, loss_inner.at[origin])
+                  for to, origin in zip(in_peers, in_from)]
+    loss_inner[me.inner] = mid
     for lo in (0, two):
         swaps[0, lo].wait_recv()
     z_up.wait_recv()
@@ -565,20 +550,14 @@
     store_q.start()
     for copy in loss_waits:
         copy.wait_recv()
-    loss_out[...] = jnp.sum(loss_inner[...], axis=0) * (1.0 / count)
+    loss_out[0, 0] = jnp.max(jnp.sum(loss_inner[...], axis=0)) * (1.0 / count)
     for copy in parts[0, 0] + parts[1, 0] + ends:
         copy.wait_recv()
     for h in (0, 1):
-        def finish(j, carry, h=h):
-            for ch, acc in enumerate(collect(h, 0, j)):
-                near_rows = slice(ch * deep, (ch + 1) * deep)
-                acc = acc + prod[ch][j, h]
-                acc = acc + last[h, 0, j, near_rows].astype(f32)
-                acc = acc + last[h, 1, j, near_rows].astype(f32)
-                pg_ref[j, h * half + ch * deep:h * half + (ch + 1) * deep] = acc.astype(b16)
-            return carry
-
-        lax.fori_loop(0, per, finish, 0)
+        for j in range(per):
+            acc = collect(h, 0, j)[0] + prod[j][h]
+            acc = acc + last[h, 0, j].astype(f32) + last[h, 1, j].astype(f32)
+            pg_ref[j, h * half:(h + 1) * half] = acc.astype(b16)
     store_p = pltpu.make_async_copy(pg_ref, pg_hbm, local.at[1])
     store_p.start()
     net.drain()
@@ -594,14 +573,14 @@
     return out
 
 
-def finish_kernel(loss_ref, q_ref, p_ref, loss_out, q_out, p_out, q_buf, p_buf, sem):
-    loads = [pltpu.make_async_copy(a, b, sem.at[i])
-             for i, (a, b) in enumerate(((q_ref, q_buf), (p_ref, p_buf)))]
-    stores = [pltpu.make_async_copy(b, a, sem.at[2 + i])
-              for i, (a, b) in enumerate(((q_out, q_buf), (p_out, p_buf)))]
+def finish_kernel(loss_ref, q_ref, p_ref, loss_out, q_out, p_out, loss_buf, q_buf, p_buf, sem):
+    moves = [(loss_ref, loss_buf, loss_out)]
+    for j in range(q_ref.shape[0]):
+        moves += [(q_ref.at[j], q_buf.at[j], q_out.at[j]), (p_ref.at[j], p_buf.at[j], p_out.at[j])]
+    loads = [pltpu.make_async_copy(a, b, sem.at[0, i]) for i, (a, b, c) in enumerate(moves)]
+    stores = [pltpu.make_async_copy(b, c, sem.at[1, i]) for i, (a, b, c) in enumerate(moves)]
     for copy in loads:
         copy.start()
-    loss_out[0, 0] = loss_ref[0, 0]
     for copy, after in zip(loads, stores):
         copy.wait()
         after.start()
@@ -632,10 +611,10 @@
         "relay": [v((chunks, 2, 2, SIDE, deep, width), b16)],
         "relay2": [v((chunks, 2, 2, SIDE, deep, width), b16)],
         "got": [v((2, slots, deep, width), b16)] * chunks,
-        "logit": [v((per, tall, full_rows), f32)] * chunks,
-        "weight": [v((per, tall, full_rows), b16)] * chunks,
-        "prod": [v((per, 2 * cands, deep, width), f32)] * chunks,
-        "cand": [v((tall, width), b16)],
+        "logit": [v((tall, full_rows), f32)] * per,
+        "weight": [v((tall, full_rows), b16)] * per,
+        "prod": [v((2 * cands, deep, width), f32)] * per,
+        "cand": [v((tall, width), b16)] * 2,
         "cols": [v((per, cands, 128), f32)],
         "row_part": [v((chunks, per, full_rows), f32)],
         "row_src": [v((per, full_rows), f32)],
@@ -673,19 +652,20 @@
     spec = {name: len(refs) for name, refs in need.items()}
     loss, query_grad, passage_grad = pl.pallas_call(
         functools.partial(fused_kernel, (chunks, groups, inners), spec),
-        out_shape=(sds((8, 128), f32), sds((per, rows, width), b16), sds((per, rows, width), b16)),
-        in_specs=[VM, AN, AN], out_specs=(VM, AN, AN),
+        out_shape=(sds((1, 1), f32), sds((per, rows, width), b16), sds((per, rows, width), b16)),
+        in_specs=[VM, AN, AN], out_specs=(SM, AN, AN),
         scratch_shapes=[ref for refs in need.values() for ref in refs],
         compiler_params=pltpu.CompilerParams(
             vmem_limit_bytes=VMEM_LIMIT, collective_id=0, has_side_effects=True),
         name="fused",
-    )(neg_lists, queries, passages)
+    )(neg_lists.T, queries, passages)
     shape = (per, rows, width)
     loss, query_grad, passage_grad = pl.pallas_call(
         finish_kernel,
         out_shape=(sds((1, 1), f32), sds(shape, b16), sds(shape, b16)),
-        in_specs=[SM, AN, AN], out_specs=(SM, AN, AN),
-        scratch_shapes=[v(shape, b16), v(shape, b16), pltpu.SemaphoreType.DMA((4,))],
+        in_specs=[AN, AN, AN], out_specs=(AN, AN, AN),
+        scratch_shapes=[pltpu.SMEM((1, 1), f32), v(shape, b16), v(shape, b16),
+                        pltpu.SemaphoreType.DMA((2, 1 + 2 * per))],
         name="finish",
     )(loss, query_grad, passage_grad)
     return (loss.reshape(()), query_grad, passage_grad)

time: 103 us -> 97.6 us (0.948)
  Pallas kernels: 101 us -> 96.6 us
  local copies, waits for them, and re-layouts: 1.38 us -> 0 us
    pallas_call x1, Pallas kernels: 97.7 us -> 93.9 us  [body(): pl.pallas_call(functools.partial(fused_kernel, (chunks, groups, inners),...]
    unnamed x1 -> x0, local copies, waits for them, and re-layouts: 1.38 us -> none
where the time goes in v4:
time: 97.6 us; the launch traced here: 97.4 us
  Pallas kernels  96.6 us (99%)
    pallas_call x1, Pallas kernels, body(): pl.pallas_call(functools.partial(fused_kernel, (chunks, groups, inners),...  93.9 us
    pallas_call x1, Pallas kernels, body(): pl.pallas_call(finish_kernel, out_shape=(sds((1, 1), f32), sds(shape, b16...  2.74 us

profile of v4, /device:TPU:0, one launch (start us, length us, event | category | flops | bytes accessed | tf_op | source)
XLA Modules:
  0.0 97.4 jit_solution(3797087886531652719)
XLA Ops:
  0.6 93.9 %fused.1 = (f32[1,1]{1,0:T(1,128)}, bf16[4,64,1024]{2,1,0:T(8,128)(2,1)}, bf16[4,64,1024]{2,1,0:T(8,128)(2,1)}) custom-call(s32[8,64]{1,0:T(8,128)} %bitcast.2, bf16[4,64,1024]{2,1,0:T(8,128)(2,1)} %q_hbm.1, bf16[4,64,1024]{2,1,0:T(8,128)(2,1)} %p_hbm.1), custom_call_target="tpu_custom_call" | custom-call | tf_op jit(solution)/shard_map/fused/pallas_call | solution.py:653
  94.5 2.7 %finish.1 = (f32[1,1]{1,0:T(1,128)}, bf16[4,64,1024]{2,1,0:T(8,128)(2,1)}, bf16[4,64,1024]{2,1,0:T(8,128)(2,1)}) custom-call(f32[1,1]{1,0:T(1,128)} %get-tuple-element.9.loss_ref, bf16[4,64,1024]{2,1,0:T(8,128)(2,1)} %get-tuple-element.10.q_ref, bf16[4,64,1024]{2,1,0:T(8,128)(2,1)} %get-tuple-element.11.p_ref), custom_call_target="tpu_custom_call" | custom-call | tf_op jit(solution)/shard_map/finish/pallas_call | solution.py:663

commit v5 on v4

--- a/solution.py
+++ b/solution.py
@@ -72,6 +72,19 @@
     return [me.move(a, s) for a in "xyz" for s in (1, -1)] + [me.move("core", 0)]
 
 
+HUBS = ((0, 1), (0, 3), (1, 1), (3, 3), (2, 3))
+TREE = (
+    ((0, 1), (0, 0), "x", 1), ((0, 3), (0, 0), "x", -1), ((1, 1), (0, 1), "y", 1),
+    ((3, 3), (0, 3), "y", -1), ((2, 3), (3, 3), "y", -1), ((1, 0), (0, 0), "y", 1),
+    ((3, 1), (0, 1), "y", -1), ((0, 2), (0, 3), "x", -1), ((1, 3), (0, 3), "y", 1),
+    ((1, 2), (1, 1), "x", 1), ((2, 1), (1, 1), "y", 1), ((3, 0), (3, 3), "x", 1),
+    ((3, 2), (3, 3), "x", -1), ((2, 0), (2, 3), "x", 1), ((2, 2), (2, 3), "x", -1))
+
+
+def turn(h, node):
+    return node if h == 0 else node[::-1]
+
+
 HALVES = (("y", "x"), ("x", "y"))
 
 
@@ -86,11 +99,12 @@
     queries = inners * rows
     slots = groups * CAP
     f32, b16 = jnp.float32, jnp.bfloat16
-    scale = 1.0 / math.sqrt(width)
+    ln2 = math.log(2.0)
+    scale = 1.0 / (math.sqrt(width) * ln2)
     count = 2.0 * groups * per * queries
     take = dict(zip(spec, split_list(scratch, spec.values())))
     one = lambda name: take[name][0]
-    full, stage, relay, relay2 = one("full"), one("stage"), one("relay"), one("relay2")
+    full, stage, relay2 = one("full"), one("stage"), one("relay2")
     got, logit, weight, prod = take["got"], take["logit"], take["weight"], take["prod"]
     cand, cols, row_part = take["cand"], one("cols"), one("row_part")
     row_src, dense_src, all_rows = one("row_src"), one("dense_src"), one("all_rows")
@@ -99,8 +113,7 @@
     dense, merge, last = one("dense"), one("merge"), one("last")
     pair_in, qsum, zmerge, zlast = one("pair_in"), one("qsum"), one("zmerge"), one("zlast")
     loss_dp, loss_inner, loss_mid = one("loss_dp"), one("loss_inner"), one("loss_mid")
-    near = [[(None,) + take["near"][(ch * 2 + h) * 3:(ch * 2 + h) * 3 + 3] for h in (0, 1)]
-            for ch in range(chunks)]
+    near = [dict(zip(HUBS, take["near"][h * len(HUBS):(h + 1) * len(HUBS)])) for h in (0, 1)]
     seen = [[take["seen"][(h * 3 + st) * SIDE:(h * 3 + st + 1) * SIDE] for st in range(3)]
             for h in (0, 1)]
     net = Copies(one("send_sem"), one("recv_sem"))
@@ -122,6 +135,64 @@
     for device in near_devices:
         pl.semaphore_signal(barrier, inc=1, device_id=device, device_id_type=MESH)
 
+    pl.semaphore_wait(barrier, len(near_devices))
+    load_p.wait()
+
+    whole = lambda h: pl.ds(h * half, half)
+    pieces = (0, two)
+    hub_in, arrivals = {}, []
+
+    def away(h, node):
+        dy, dx = turn(h, node)
+        return mod4(me.y + dy) * SIDE + mod4(me.x + dx)
+
+    def toward(h, axis, step):
+        return me.move(axis if h == 0 else {"x": "y", "y": "x"}[axis], step)
+
+    def slot_from(h, node):
+        dy, dx = turn(h, node)
+        return ((-dy % SIDE) * SIDE + (-dx % SIDE)) * CAP
+
+    def feed(h, parent, lo):
+        for node, up, axis, step in TREE:
+            if up == parent and node in HUBS:
+                src = p_ref.at[pl.ds(lo, two), whole(h)] if parent == (0, 0) else (
+                    near[h][parent].at[pl.ds(lo, two)])
+                hub_in[h, node, lo] = net.send(
+                    src, near[h][node].at[pl.ds(lo, two)], toward(h, axis, step))
+
+    def await_hub(h, node, lo):
+        hub_in[h, node, lo].wait_recv()
+
+    def pick_block(h, parent, group, c):
+        back = tuple(-v % SIDE for v in parent)
+        pick = pick_of(group, away(h, back), c)
+        return p_ref[pick, whole(h)] if parent == (0, 0) else near[h][parent][pick]
+
+    def serve(h, parent):
+        for n, (node, up, axis, step) in enumerate(TREE):
+            if up != parent or node in HUBS:
+                continue
+            hop = tuple((a - b) % SIDE for a, b in zip(node, up))
+            group = away(h, hop)
+            for c in range(CAP):
+                stage[h, n - len(HUBS), c] = pick_block(h, parent, group, c)
+            arrivals.append(net.send(
+                stage.at[h, n - len(HUBS)], got[0].at[h, pl.ds(slot_from(h, node), CAP)],
+                toward(h, axis, step)))
+
+    def keep_own(h, node):
+        for c in range(CAP):
+            got[0][h, slot_from(h, node) + c] = pick_block(h, node, me.dp, c)
+
+    at = lambda z, c: full.at[mod4(z) * 2 + c]
+    for lo in pieces:
+        for h in (0, 1):
+            feed(h, (0, 0), lo)
+    load_q.wait()
+    z_up = net.send(own_slot, own_slot, me.move("z", 1), at(me.z - 1, me.c))
+    z_down = net.send(own_slot, own_slot, me.move("z", -1), at(me.z + 1, me.c))
+    pair = [net.send(own_slot, own_slot, me.move("core", 0), at(me.z, 1 - me.c))]
     tab_v, tab_s, spot_v, spot_s = one("tab_v"), one("tab_s"), one("spot_v"), one("spot_s")
     blocks = list_ref.shape[1]
     every = jnp.transpose(jnp.concatenate(
@@ -160,77 +231,23 @@
     def listed(b, k):
         return spot_s[b, blocks + k]
 
-    pl.semaphore_wait(barrier, len(near_devices))
-    load_p.wait()
-
-    span = lambda h, ch: pl.ds(h * half + ch * deep, deep)
-    first, second, relays, arrivals = {}, {}, {}, {ch: [] for ch in range(chunks)}
-
-    def send_own(ch):
-        for h, (f, t) in enumerate(HALVES):
-            mine = p_ref.at[:, span(h, ch)]
-            first[ch, h] = (net.send(mine, near[ch][h][3], me.move(f, 1)),
-                            net.send(mine, near[ch][h][1], me.move(f, -1)))
-
-    def send_second(ch):
-        for h, (f, t) in enumerate(HALVES):
-            up, down = first[ch, h]
-            up.wait_recv()
-            a = net.send(near[ch][h][3].at[0:two], near[ch][h][2].at[0:two], me.move(f, 1))
-            down.wait_recv()
-            b = net.send(near[ch][h][1].at[two:per], near[ch][h][2].at[two:per], me.move(f, -1))
-            second[ch, h] = (a, b)
-
-    def spread(ch, rf):
-        for h, (f, t) in enumerate(HALVES):
-            if rf == 2:
-                for copy in second[ch, h]:
-                    copy.wait_recv()
-            source = me.group(f, rf, 0)
-            for dt in (2, 1, 3, 0):
-                if dt == 0 and rf == 0:
-                    got[ch][h, 0:CAP] = jnp.zeros((CAP, deep, width), b16)
-                    continue
-                group = me.group(f, 0, dt)
-                for c in range(CAP):
-                    pick = pick_of(group, source, c)
-                    block = p_ref[pick, span(h, ch)] if rf == 0 else near[ch][h][rf][pick]
-                    if dt == 0:
-                        got[ch][h, rf * CAP + c] = block
-                    else:
-                        stage[ch, h, dt - 1, rf, c] = block
-            up, down = me.move(t, 1), me.move(t, -1)
-            relays[ch, h, rf] = (
-                net.send(stage.at[ch, h, 1, rf, 0], relay.at[ch, h, 0, rf], up),
-                net.send(stage.at[ch, h, 1, rf, 1], relay.at[ch, h, 1, rf], down))
-            arrivals[ch].append(net.send(
-                stage.at[ch, h, 0, rf], got[ch].at[h, pl.ds(24 + rf * CAP, CAP)], up))
-            arrivals[ch].append(net.send(
-                stage.at[ch, h, 2, rf], got[ch].at[h, pl.ds(8 + rf * CAP, CAP)], down))
-
-    def pass_on(ch, *rfs):
-        for rf in rfs:
-            for h, (f, t) in enumerate(HALVES):
-                for side, copy in enumerate(relays[ch, h, rf]):
-                    copy.wait_recv()
-                    arrivals[ch].append(net.send(
-                        relay.at[ch, h, side, rf], got[ch].at[h, 16 + rf * CAP + side],
-                        me.move(t, 1 - 2 * side)))
-
-    at = lambda z, c: full.at[mod4(z) * 2 + c]
-    send_own(0)
-    load_q.wait()
-    z_up = net.send(own_slot, own_slot, me.move("z", 1), at(me.z - 1, me.c))
-    z_down = net.send(own_slot, own_slot, me.move("z", -1), at(me.z + 1, me.c))
-    pair = [net.send(own_slot, own_slot, me.move("core", 0), at(me.z, 1 - me.c))]
     tab_copy.wait()
     spot_copy.wait()
-    spread(0, 0)
-    for ch in range(1, chunks):
-        send_own(ch)
-    send_second(0)
-    spread(0, 1)
-    spread(0, 3)
+    for h in (0, 1):
+        serve(h, (0, 0))
+        got[0][h, 0:CAP] = jnp.zeros((CAP, half, width), b16)
+    for lo in pieces:
+        for node in ((0, 3), (0, 1)):
+            for h in (0, 1):
+                await_hub(h, node, lo)
+                feed(h, node, lo)
+    for node in ((0, 3), (0, 1)):
+        for h in (0, 1):
+            serve(h, node)
+    for lo in pieces:
+        for h in (0, 1):
+            await_hub(h, (3, 3), lo)
+            feed(h, (3, 3), lo)
     z_up.wait_recv()
     behind, ahead = at(me.z - 1, me.c), at(me.z + 1, me.c)
     across = mod4(me.z + 2) * 2
@@ -240,27 +257,22 @@
     z_down.wait_recv()
     zb = net.send(ahead.at[two:per], ahead.at[two:per], me.move("z", -1), far.at[two:per])
     pair.append(net.send(ahead, ahead, me.move("core", 0), at(me.z + 1, 1 - me.c)))
-    pass_on(0, 0)
-    for ch in range(1, chunks):
-        send_second(ch)
-    spread(0, 2)
-    for ch in range(1, chunks):
-        spread(ch, 0)
-        pass_on(ch - 1, 1, 3)
-        spread(ch, 1)
-        spread(ch, 3)
-        if ch == 1:
-            za.wait_recv()
-            zb.wait_recv()
-            pair.append(
-                net.send(far, far, me.move("core", 0), full.at[across + 1 - me.c]))
-        pass_on(ch - 1, 2)
-        spread(ch, 2)
-        pass_on(ch, 0)
-    if chunks == 1:
-        za.wait_recv()
-        zb.wait_recv()
-        pair.append(net.send(far, far, me.move("core", 0), full.at[across + 1 - me.c]))
+    for h in (0, 1):
+        serve(h, (3, 3))
+    for h in (0, 1):
+        for lo in pieces:
+            await_hub(h, (1, 1), lo)
+        serve(h, (1, 1))
+    for h in (0, 1):
+        for lo in pieces:
+            await_hub(h, (2, 3), lo)
+        serve(h, (2, 3))
+    za.wait_recv()
+    zb.wait_recv()
+    pair.append(net.send(far, far, me.move("core", 0), full.at[across + 1 - me.c]))
+    for node in HUBS:
+        for h in (0, 1):
+            keep_own(h, node)
 
     lane = lax.broadcasted_iota(jnp.int32, (2 * deep, 128), 1)
     sub = lax.broadcasted_iota(jnp.int32, (2 * deep, 128), 0)
@@ -281,8 +293,9 @@
             ry = mod4(group // SIDE - me.y)
             rx = mod4(lax.rem(group, SIDE) - me.x)
             base = rows * (k + 1)
-            to[base:base + half] = got[0][0, rx * 8 + ry * 2 + r]
-            to[base + half:base + rows] = got[0][1, ry * 8 + rx * 2 + r]
+            slot = (ry * SIDE + rx) * CAP + r
+            to[base:base + half] = got[0][0, slot]
+            to[base + half:base + rows] = got[0][1, slot]
 
     def score(b):
         load_candidates(b)
@@ -290,28 +303,35 @@
         logit[b][...] = lax.dot_general(
             cand[b % 2][...], q, (((1,), (1,)), ((), ())), preferred_element_type=f32) * scale
 
+    line = lax.broadcasted_iota(jnp.int32, (32, 128), 0)
+    side = lax.broadcasted_iota(jnp.int32, (32, 128), 1) // 64
+    home = line + 32 * side
+
+    def block_of(b, i):
+        return me.dp * per + b if i == 0 else listed(b, i - 1)
+
     def summarise(b):
         peak = jnp.full((1, queries), NEG, f32)
+        placed = jnp.full((32, 128), NEG, f32)
         for i in range(cands):
             block = logit[b][i * rows:(i + 1) * rows]
             peak = jnp.maximum(peak, jnp.max(block, axis=0, keepdims=True))
             top = jnp.max(block, axis=1, keepdims=True)
-            lse = top + jnp.log(jnp.sum(jnp.exp(block - top), axis=1, keepdims=True))
+            lse = top + jnp.log2(jnp.sum(jnp.exp2(block - top), axis=1, keepdims=True))
             if i == 0:
                 hit = wide_lane == wide_sub + me.inner * rows
                 own_sum[...] += jnp.sum(jnp.where(hit, block, 0.0))
-            cols[b, i:i + 1] = jnp.sum(jnp.where(lax.rem(lane, 64) == sub, lse, 0.0), axis=0,
-                                       keepdims=True)
+            line_of = jnp.sum(jnp.where(lax.rem(lane, 64) == sub, lse, 0.0), axis=0, keepdims=True)
+            placed = jnp.where(home == block_of(b, i), line_of, placed)
+        cols[b] = placed
         total = jnp.zeros((1, queries), f32)
         for i in range(cands):
             block = logit[b][i * rows:(i + 1) * rows]
-            total = total + jnp.sum(jnp.exp(block - peak), axis=0, keepdims=True)
-        row_part[0, b:b + 1] = peak + jnp.log(total)
+            total = total + jnp.sum(jnp.exp2(block - peak), axis=0, keepdims=True)
+        row_part[0, b:b + 1] = peak + jnp.log2(total)
 
     own_sum[...] = jnp.zeros(own_sum.shape, f32)
-    pass_on(0, 1, 3)
-    pass_on(0, 2)
-    for copy in arrivals[0] + pair:
+    for copy in arrivals + pair:
         copy.wait_recv()
     score(0)
     for b in range(1, per):
@@ -321,33 +341,13 @@
 
     def fold(values):
         top = jnp.max(values, axis=0)
-        return top + jnp.log(jnp.sum(jnp.exp(values - top[None]), axis=0))
-
-    rows_mine = fold(row_part[...])
+        return top + jnp.log2(jnp.sum(jnp.exp2(values - top[None]), axis=0))
+
+    rows_mine = row_part[0]
     row_src[...] = rows_mine
     stat_waits = [net.send(row_src, all_rows.at[me.inner], to, all_rows.at[origin])
                   for to, origin in zip(in_peers, in_from)]
-    line = lax.broadcasted_iota(jnp.int32, (32, 128), 0)
-    side = lax.broadcasted_iota(jnp.int32, (32, 128), 1) // 64
-    home = line + 32 * side
-
-    def block_of(b, i):
-        return me.dp * per + b if i == 0 else listed(b, i - 1)
-
-    def raise_peak(b, peak):
-        for i in range(cands):
-            peak = jnp.where(home == block_of(b, i), jnp.maximum(peak, cols[b, i:i + 1]), peak)
-        return peak
-
-    peaks = lax.fori_loop(0, per, raise_peak, jnp.full((32, 128), NEG, f32))
-
-    def add_mass(b, mass):
-        for i in range(cands):
-            mass = mass + jnp.where(home == block_of(b, i), jnp.exp(cols[b, i:i + 1] - peaks), 0.0)
-        return mass
-
-    mass = lax.fori_loop(0, per, add_mass, jnp.zeros((32, 128), f32))
-    dense_mine = jnp.where(mass > 0.0, peaks + jnp.log(jnp.where(mass > 0.0, mass, 1.0)), NEG)
+    dense_mine = fold(cols[...])
     dense_src[...] = dense_mine
     stat_waits += [net.send(dense_src, all_dense.at[me.dp], to, all_dense.at[origin])
                    for to, origin in zip(dp_peers, dp_from)]
@@ -364,14 +364,14 @@
     loss_mid[0] = loss_own - 2.0 * own_sum[...]
 
     def weigh(b):
-        row = row_lse[b:b + 1]
+        row = row_lse[b:b + 1] + 1.0
         for i in range(cands):
             block = block_of(b, i)
             values = pass_lse[pl.ds(lax.rem(block, 32), 1)]
             pick = lane == sub + (block // 32) * 64
-            col = jnp.sum(jnp.where(pick, values, 0.0), axis=1, keepdims=True)
+            col = jnp.sum(jnp.where(pick, values, 0.0), axis=1, keepdims=True) + 1.0
             z = logit[b][i * rows:(i + 1) * rows]
-            probs = 0.5 * jnp.exp(z - row) + 0.5 * jnp.exp(z - col)
+            probs = jnp.exp2(z - row) + jnp.exp2(z - col)
             if i == 0:
                 hit = wide_lane == wide_sub + me.inner * rows
                 probs = probs - jnp.where(hit, 1.0, 0.0)
@@ -452,22 +452,15 @@
 
         lax.fori_loop(0, two, step, 0)
 
-    def collect(h, rf, j):
+    def collect(h, rf, j, sources, acc):
         f, t = HALVES[h]
         owner = me.group(f, rf, 0)
-        acc = [jnp.zeros((deep, width), f32) for _ in range(chunks)]
-        for st in range(SIDE):
-            if st == 0 and rf == 0:
-                continue
+        for st in sources:
             r = rank_of(me.group(f, 0, st), owner * per + j)
             live = (r >= 0).astype(f32)
             c = jnp.maximum(r, 0)
-            for ch in range(chunks):
-                if st == 0:
-                    block = part[ch, h, rf * CAP + c]
-                else:
-                    block = seen[h][st - 1][rf][c, ch * deep:(ch + 1) * deep]
-                acc[ch] = acc[ch] + block.astype(f32) * live
+            block = part[0, h, rf * CAP + c] if st == 0 else seen[h][st - 1][rf][c]
+            acc = acc + block.astype(f32) * live
         return acc
 
     def gather_parts(h, rf):
@@ -475,8 +468,8 @@
             copy.wait_recv()
 
         def step(j, carry):
-            for ch, acc in enumerate(collect(h, rf, j)):
-                dense[h, rf - 1, j, ch * deep:(ch + 1) * deep] = acc.astype(b16)
+            acc = collect(h, rf, j, range(SIDE), jnp.zeros((half, width), f32))
+            dense[h, rf - 1, j] = acc.astype(b16)
             return carry
 
         lax.fori_loop(0, per, step, 0)
@@ -528,6 +521,11 @@
             ends.append(net.send(dense.at[h, rf - 1], last.at[h, slot],
                                  me.move(f, 1 if slot == 0 else -1)))
     forward_parts(0, 0)
+    for h in (0, 1):
+        for copy in parts[h, 0][:2]:
+            copy.wait_recv()
+        for j in range(per):
+            prod[j][h] = collect(h, 0, j, (1, 3), prod[j][h])
     for copy in loss_waits:
         copy.wait_recv()
     mid = jnp.sum(loss_dp[...], axis=0)
@@ -550,19 +548,24 @@
     store_q.start()
     for copy in loss_waits:
         copy.wait_recv()
-    loss_out[0, 0] = jnp.max(jnp.sum(loss_inner[...], axis=0)) * (1.0 / count)
-    for copy in parts[0, 0] + parts[1, 0] + ends:
+    loss_out[0, 0] = jnp.max(jnp.sum(loss_inner[...], axis=0)) * (ln2 / count)
+    for h in (0, 1):
+        for copy in parts[h, 0][2:]:
+            copy.wait_recv()
+    for copy in ends:
         copy.wait_recv()
-    for h in (0, 1):
-        for j in range(per):
-            acc = collect(h, 0, j)[0] + prod[j][h]
+    store_p = []
+    for j in range(per):
+        for h in (0, 1):
+            acc = collect(h, 0, j, (2,), prod[j][h])
             acc = acc + last[h, 0, j].astype(f32) + last[h, 1, j].astype(f32)
             pg_ref[j, h * half:(h + 1) * half] = acc.astype(b16)
-    store_p = pltpu.make_async_copy(pg_ref, pg_hbm, local.at[1])
-    store_p.start()
+        store_p.append(pltpu.make_async_copy(pg_ref.at[j], pg_hbm.at[j], local.at[4 + j]))
+        store_p[-1].start()
     net.drain()
     store_q.wait()
-    store_p.wait()
+    for copy in store_p:
+        copy.wait()
 
 
 def split_list(items, counts):
@@ -607,15 +610,14 @@
     sem_count = 100 + 160 * chunks
     need = {
         "full": [v((inners, per, rows, width), b16)],
-        "stage": [v((chunks, 2, SIDE - 1, SIDE, CAP, deep, width), b16)],
-        "relay": [v((chunks, 2, 2, SIDE, deep, width), b16)],
+        "stage": [v((2, len(TREE) - len(HUBS), CAP, half, width), b16)],
         "relay2": [v((chunks, 2, 2, SIDE, deep, width), b16)],
         "got": [v((2, slots, deep, width), b16)] * chunks,
         "logit": [v((tall, full_rows), f32)] * per,
         "weight": [v((tall, full_rows), b16)] * per,
         "prod": [v((2 * cands, deep, width), f32)] * per,
         "cand": [v((tall, width), b16)] * 2,
-        "cols": [v((per, cands, 128), f32)],
+        "cols": [v((per, 32, 128), f32)],
         "row_part": [v((chunks, per, full_rows), f32)],
         "row_src": [v((per, full_rows), f32)],
         "dense_src": [v((32, 128), f32)],
@@ -636,11 +638,11 @@
         "loss_dp": [v((groups, 8, 128), f32)],
         "loss_inner": [v((inners, 8, 128), f32)],
         "loss_mid": [v((2, 8, 128), f32)],
-        "near": [v((per, deep, width), b16)] * (2 * 3 * chunks),
+        "near": [v((per, half, width), b16)] * (2 * len(HUBS)),
         "seen": [v((CAP, half, width), b16)] * (2 * 3 * SIDE),
         "send_sem": [pltpu.SemaphoreType.DMA((sem_count,))],
         "recv_sem": [pltpu.SemaphoreType.DMA((sem_count,))],
-        "local_sem": [pltpu.SemaphoreType.DMA((4,))],
+        "local_sem": [pltpu.SemaphoreType.DMA((4 + per,))],
         "p_own": [v((per, rows, width), b16)],
         "qg": [v((per, rows, width), b16)],
         "pg": [v((per, rows, width), b16)],

time: 97.6 us -> 94.1 us (0.964)
  Pallas kernels: 96.6 us -> 92.9 us
    pallas_call x1, Pallas kernels: 93.9 us -> 90.2 us  [body(): pl.pallas_call(functools.partial(fused_kernel, (chunks, groups, inners),...]
where the time goes in v5:
time: 94.1 us; the launch traced here: 93.7 us
  Pallas kernels  92.9 us (99%)
    pallas_call x1, Pallas kernels, body(): pl.pallas_call(functools.partial(fused_kernel, (chunks, groups, inners),...  90.2 us
    pallas_call x1, Pallas kernels, body(): pl.pallas_call(finish_kernel, out_shape=(sds((1, 1), f32), sds(shape, b16...  2.74 us

profile of v5, /device:TPU:0, one launch (start us, length us, event | category | flops | bytes accessed | tf_op | source)
XLA Modules:
  0.0 93.7 jit_solution(17112433808418177460)
XLA Ops:
  0.6 90.2 %fused.1 = (f32[1,1]{1,0:T(1,128)}, bf16[4,64,1024]{2,1,0:T(8,128)(2,1)}, bf16[4,64,1024]{2,1,0:T(8,128)(2,1)}) custom-call(s32[8,64]{1,0:T(8,128)} %bitcast.2, bf16[4,64,1024]{2,1,0:T(8,128)(2,1)} %q_hbm.1, bf16[4,64,1024]{2,1,0:T(8,128)(2,1)} %p_hbm.1), custom_call_target="tpu_custom_call" | custom-call | tf_op jit(solution)/shard_map/fused/pallas_call | solution.py:655
  90.8 2.7 %finish.1 = (f32[1,1]{1,0:T(1,128)}, bf16[4,64,1024]{2,1,0:T(8,128)(2,1)}, bf16[4,64,1024]{2,1,0:T(8,128)(2,1)}) custom-call(f32[1,1]{1,0:T(1,128)} %get-tuple-element.9.loss_ref, bf16[4,64,1024]{2,1,0:T(8,128)(2,1)} %get-tuple-element.10.q_ref, bf16[4,64,1024]{2,1,0:T(8,128)(2,1)} %get-tuple-element.11.p_ref), custom_call_target="tpu_custom_call" | custom-call | tf_op jit(solution)/shard_map/finish/pallas_call | solution.py:665

commit v6 on v5

--- a/solution.py
+++ b/solution.py
@@ -104,18 +104,19 @@
     count = 2.0 * groups * per * queries
     take = dict(zip(spec, split_list(scratch, spec.values())))
     one = lambda name: take[name][0]
-    full, stage, relay2 = one("full"), one("stage"), one("relay2")
+    full, stage = one("full"), one("stage")
     got, logit, weight, prod = take["got"], take["logit"], take["weight"], take["prod"]
     cand, cols, row_part = take["cand"], one("cols"), one("row_part")
     row_src, dense_src, all_rows = one("row_src"), one("dense_src"), one("all_rows")
     all_dense, row_lse, pass_lse = one("all_dense"), one("row_lse"), one("pass_lse")
     part, query_part, own_sum = one("part"), one("query_part"), one("own_sum")
-    dense, merge, last = one("dense"), one("merge"), one("last")
+    dense = one("dense")
     pair_in, qsum, zmerge, zlast = one("pair_in"), one("qsum"), one("zmerge"), one("zlast")
     loss_dp, loss_inner, loss_mid = one("loss_dp"), one("loss_inner"), one("loss_mid")
     near = [dict(zip(HUBS, take["near"][h * len(HUBS):(h + 1) * len(HUBS)])) for h in (0, 1)]
-    seen = [[take["seen"][(h * 3 + st) * SIDE:(h * 3 + st + 1) * SIDE] for st in range(3)]
-            for h in (0, 1)]
+    leaves = [node for node, *_ in TREE if node not in HUBS]
+    seen = [dict(zip(leaves, take["seen"][h * len(leaves):])) for h in (0, 1)]
+    hub_sum = [dict(zip(HUBS, take["hub_sum"][h * len(HUBS):])) for h in (0, 1)]
     net = Copies(one("send_sem"), one("recv_sem"))
 
     dp_peers = [(lax.rem(me.dp + o, groups), me.inner) for o in range(1, groups)]
@@ -382,43 +383,77 @@
         out = jnp.dot(weight[b][...], q, preferred_element_type=f32)
         prod[b][...] = out.reshape(2 * cands, deep, width)
 
-    send_rows, parts = {}, {(h, rf): [] for h in (0, 1) for rf in range(SIDE)}
-
-    def emit(ch, rf):
-        for h, (f, t) in enumerate(HALVES):
-            def slot(i, carry, h=h, f=f):
-                rt, c = i // CAP, lax.rem(i, CAP)
-                owner = me.group(f, rf, rt)
-                block = owner * per + jnp.where(
-                    c == 0, pick_of(me.dp, owner, 0), pick_of(me.dp, owner, 1))
-                acc = jnp.zeros((deep, width), f32)
-                for b in range(per):
-                    k = spot_s[b, block]
-                    live = (k >= 0).astype(f32)
-                    acc = acc + prod[b][2 * (jnp.maximum(k, 0) + 1) + h] * live
-                part[ch, h, rt * 8 + rf * CAP + c] = acc.astype(b16)
-                return carry
-
-            lax.fori_loop(CAP if rf == 0 else 0, SIDE * CAP, slot, 0)
-            up, down = me.move(t, 1), me.move(t, -1)
-            rel = pl.ds(ch * deep, deep)
-            send_rows[ch, h, rf] = (
-                net.send(part.at[ch, h, 16 + rf * CAP], relay2.at[ch, h, 0, rf], up),
-                net.send(part.at[ch, h, 16 + rf * CAP + 1], relay2.at[ch, h, 1, rf], down))
-            parts[h, rf] += [
-                net.send(part.at[ch, h, pl.ds(8 + rf * CAP, CAP)], seen[h][2][rf].at[:, rel], up),
-                net.send(part.at[ch, h, pl.ds(24 + rf * CAP, CAP)], seen[h][0][rf].at[:, rel],
-                         down)]
-
-    def forward_parts(ch, *rfs):
-        for rf in rfs:
-            for h, (f, t) in enumerate(HALVES):
-                for side_, copy in enumerate(send_rows[ch, h, rf]):
-                    copy.wait_recv()
-                    parts[h, rf].append(net.send(
-                        relay2.at[ch, h, side_, rf],
-                        seen[h][1][rf].at[side_, pl.ds(ch * deep, deep)],
-                        me.move(t, 1 - 2 * side_)))
+    part_in, sum_in = {}, {}
+
+    def back_of(node):
+        return tuple(-v % SIDE for v in node)
+
+    def make(h, node):
+        owner = away(h, back_of(node))
+
+        def slot(c, carry):
+            block = owner * per + jnp.where(
+                c == 0, pick_of(me.dp, owner, 0), pick_of(me.dp, owner, 1))
+            acc = jnp.zeros((half, width), f32)
+            for b in range(per):
+                k = spot_s[b, block]
+                live = (k >= 0).astype(f32)
+                acc = acc + prod[b][2 * (jnp.maximum(k, 0) + 1) + h] * live
+            part[0, h, slot_from(h, node) + c] = acc.astype(b16)
+            return carry
+
+        lax.fori_loop(0, CAP, slot, 0)
+
+    def emit(*nodes):
+        for node, up, axis, step in TREE:
+            if node in nodes:
+                for h in (0, 1):
+                    make(h, node)
+                    part_in[h, node] = net.send(
+                        part.at[0, h, pl.ds(slot_from(h, node), CAP)], seen[h][node],
+                        toward(h, axis, -step))
+
+    def collect(h, here, j, acc):
+        block = away(h, back_of(here)) * per + j
+        if here != (0, 0):
+            r = rank_of(me.dp, block)
+            mine_ = part[0, h, slot_from(h, here) + jnp.maximum(r, 0)]
+            acc = acc + mine_.astype(f32) * (r >= 0).astype(f32)
+        for node, up, axis, step in TREE:
+            if up != here:
+                continue
+            if node in HUBS:
+                acc = acc + hub_sum[h][node][j].astype(f32)
+            else:
+                hop = tuple((a - b) % SIDE for a, b in zip(node, up))
+                r = rank_of(away(h, hop), block)
+                piece = seen[h][node][jnp.maximum(r, 0)]
+                acc = acc + piece.astype(f32) * (r >= 0).astype(f32)
+        return acc
+
+    def climb(*here):
+        for lo in pieces:
+            for at_hub in here:
+                for h in (0, 1):
+                    climb_piece(h, at_hub, lo)
+
+    def climb_piece(h, here, lo):
+        n = HUBS.index(here)
+        axis, step = [(a, s) for node, _, a, s in TREE if node == here][0]
+        for node, up, *_ in TREE:
+            if up == here and node in HUBS:
+                sum_in[h, node, lo].wait_recv()
+            elif up == here and lo == 0:
+                part_in[h, node].wait_recv()
+
+        def block(j, carry):
+            dense[h, n, j] = collect(h, here, j, jnp.zeros((half, width), f32)).astype(b16)
+            return carry
+
+        lax.fori_loop(lo, lo + two, block, 0)
+        sum_in[h, here, lo] = net.send(
+            dense.at[h, n, pl.ds(lo, two)], hub_sum[h][here].at[pl.ds(lo, two)],
+            toward(h, axis, -step))
 
     def query_grad(b):
         load_candidates(b)
@@ -452,80 +487,54 @@
 
         lax.fori_loop(0, two, step, 0)
 
-    def collect(h, rf, j, sources, acc):
-        f, t = HALVES[h]
-        owner = me.group(f, rf, 0)
-        for st in sources:
-            r = rank_of(me.group(f, 0, st), owner * per + j)
-            live = (r >= 0).astype(f32)
-            c = jnp.maximum(r, 0)
-            block = part[0, h, rf * CAP + c] if st == 0 else seen[h][st - 1][rf][c]
-            acc = acc + block.astype(f32) * live
-        return acc
-
-    def gather_parts(h, rf):
-        for copy in parts[h, rf]:
-            copy.wait_recv()
-
-        def step(j, carry):
-            acc = collect(h, rf, j, range(SIDE), jnp.zeros((half, width), f32))
-            dense[h, rf - 1, j] = acc.astype(b16)
-            return carry
-
-        lax.fori_loop(0, per, step, 0)
-
-    merges, ends = {}, []
     weigh(0)
     for b in range(1, per):
         multiply(b - 1)
         weigh(b)
     multiply(per - 1)
-    emit(0, 2)
-    emit(0, 1)
+    emit((2, 0), (2, 2))
+    emit((3, 0), (3, 2))
+    query_grad(0)
+    emit((1, 2), (2, 1))
     loss_waits = [net.send(loss_mid.at[0], loss_dp.at[me.dp], to, loss_dp.at[origin])
                   for to, origin in zip(dp_peers, dp_from)]
     loss_dp[me.dp] = loss_mid[0]
-    for b in range(0, two):
-        query_grad(b)
+    for h in (0, 1):
+        make(h, (2, 3))
+    climb((2, 3))
+    query_grad(1)
     swap(0)
-    forward_parts(0, 2)
-    emit(0, 3)
     for b in range(two, per):
         query_grad(b)
     swap(two)
-    forward_parts(0, 1)
+    emit((0, 2), (1, 3), (3, 1))
     join(2, 0)
     za = net.send(qsum.at[2, 0:two], zmerge.at[0], me.move("z", 1))
     join(2, two)
     zb = net.send(qsum.at[2, two:per], zmerge.at[1], me.move("z", -1))
-    forward_parts(0, 3)
-    for h, (f, t) in enumerate(HALVES):
-        gather_parts(h, 2)
-        merges[h] = [net.send(dense.at[h, 1, 0:two], merge.at[h, 0], me.move(f, 1)),
-                     net.send(dense.at[h, 1, two:per], merge.at[h, 1], me.move(f, -1))]
-    emit(0, 0)
-    for lo in (0, two):
-        join(1, lo)
-        join(3, lo)
+    for h in (0, 1):
+        make(h, (3, 3))
+    climb((3, 3))
+    join(1, two)
+    z_in = [net.send(qsum.at[1, two:per], zlast.at[0, two:per], me.move("z", 1))]
+    join(3, 0)
+    z_in.append(net.send(qsum.at[3, 0:two], zlast.at[1, 0:two], me.move("z", -1)))
+    for h in (0, 1):
+        make(h, (1, 1))
+    climb((1, 1))
+    emit((1, 0))
+    join(1, 0)
+    join(3, two)
+    for h in (0, 1):
+        make(h, (0, 3))
+        make(h, (0, 1))
     za.wait_recv()
     fold_in(qsum, 1, zmerge.at[0], 0)
-    z_up = net.send(qsum.at[1], zlast.at[0], me.move("z", 1))
+    z_in.append(net.send(qsum.at[1, 0:two], zlast.at[0, 0:two], me.move("z", 1)))
     zb.wait_recv()
     fold_in(qsum, 3, zmerge.at[1], two)
-    z_down = net.send(qsum.at[3], zlast.at[1], me.move("z", -1))
-    for rf, slot in ((1, 0), (3, 1)):
-        for h, (f, t) in enumerate(HALVES):
-            gather_parts(h, rf)
-            merges[h][slot].wait_recv()
-            fold_in(dense.at[h], rf - 1, merge.at[h, slot], slot * two)
-            ends.append(net.send(dense.at[h, rf - 1], last.at[h, slot],
-                                 me.move(f, 1 if slot == 0 else -1)))
-    forward_parts(0, 0)
-    for h in (0, 1):
-        for copy in parts[h, 0][:2]:
-            copy.wait_recv()
-        for j in range(per):
-            prod[j][h] = collect(h, 0, j, (1, 3), prod[j][h])
+    z_in.append(net.send(qsum.at[3, two:per], zlast.at[1, two:per], me.move("z", -1)))
+    climb((0, 3), (0, 1))
     for copy in loss_waits:
         copy.wait_recv()
     mid = jnp.sum(loss_dp[...], axis=0)
@@ -535,8 +544,8 @@
     loss_inner[me.inner] = mid
     for lo in (0, two):
         swaps[0, lo].wait_recv()
-    z_up.wait_recv()
-    z_down.wait_recv()
+    for copy in z_in:
+        copy.wait_recv()
     def finish_query(j, carry):
         both = query_part[mine, j].astype(f32) + pair_in[0, j].astype(f32)
         both = both + zlast[0, j].astype(f32) + zlast[1, j].astype(f32)
@@ -550,15 +559,14 @@
         copy.wait_recv()
     loss_out[0, 0] = jnp.max(jnp.sum(loss_inner[...], axis=0)) * (ln2 / count)
     for h in (0, 1):
-        for copy in parts[h, 0][2:]:
-            copy.wait_recv()
-    for copy in ends:
-        copy.wait_recv()
+        part_in[h, (1, 0)].wait_recv()
     store_p = []
     for j in range(per):
         for h in (0, 1):
-            acc = collect(h, 0, j, (2,), prod[j][h])
-            acc = acc + last[h, 0, j].astype(f32) + last[h, 1, j].astype(f32)
+            if j in pieces:
+                for node in ((0, 3), (0, 1)):
+                    sum_in[h, node, j].wait_recv()
+            acc = collect(h, (0, 0), j, prod[j][h])
             pg_ref[j, h * half:(h + 1) * half] = acc.astype(b16)
         store_p.append(pltpu.make_async_copy(pg_ref.at[j], pg_hbm.at[j], local.at[4 + j]))
         store_p[-1].start()
@@ -611,7 +619,6 @@
     need = {
         "full": [v((inners, per, rows, width), b16)],
         "stage": [v((2, len(TREE) - len(HUBS), CAP, half, width), b16)],
-        "relay2": [v((chunks, 2, 2, SIDE, deep, width), b16)],
         "got": [v((2, slots, deep, width), b16)] * chunks,
         "logit": [v((tall, full_rows), f32)] * per,
         "weight": [v((tall, full_rows), b16)] * per,
@@ -628,9 +635,8 @@
         "part": [v((chunks, 2, slots, deep, width), b16)],
         "query_part": [v((inners, per, rows, width), b16)],
         "own_sum": [v((8, 128), f32)],
-        "dense": [v((2, SIDE - 1, per, half, width), b16)],
-        "merge": [v((2, 2, two, half, width), b16)],
-        "last": [v((2, 2, per, half, width), b16)],
+        "dense": [v((2, len(HUBS), per, half, width), b16)],
+        "hub_sum": [v((per, half, width), b16)] * (2 * len(HUBS)),
         "pair_in": [v((SIDE, per, rows, width), b16)],
         "qsum": [v((SIDE, per, rows, width), b16)],
         "zmerge": [v((2, two, rows, width), b16)],
@@ -639,7 +645,7 @@
         "loss_inner": [v((inners, 8, 128), f32)],
         "loss_mid": [v((2, 8, 128), f32)],
         "near": [v((per, half, width), b16)] * (2 * len(HUBS)),
-        "seen": [v((CAP, half, width), b16)] * (2 * 3 * SIDE),
+        "seen": [v((CAP, half, width), b16)] * (2 * (len(TREE) - len(HUBS))),
         "send_sem": [pltpu.SemaphoreType.DMA((sem_count,))],
         "recv_sem": [pltpu.SemaphoreType.DMA((sem_count,))],
         "local_sem": [pltpu.SemaphoreType.DMA((4 + per,))],

time: 94.1 us -> 92 us (0.978)
  Pallas kernels: 92.9 us -> 90.8 us
    pallas_call x1, Pallas kernels: 90.2 us -> 88.1 us  [body(): pl.pallas_call(functools.partial(fused_kernel, (chunks, groups, inners),...]
where the time goes in v6:
time: 92 us; the launch traced here: 91.6 us
  Pallas kernels  90.8 us (99%)
    pallas_call x1, Pallas kernels, body(): pl.pallas_call(functools.partial(fused_kernel, (chunks, groups, inners),...  88.1 us
    pallas_call x1, Pallas kernels, body(): pl.pallas_call(finish_kernel, out_shape=(sds((1, 1), f32), sds(shape, b16...  2.74 us

profile of v6, /device:TPU:0, one launch (start us, length us, event | category | flops | bytes accessed | tf_op | source)
XLA Modules:
  0.0 91.6 jit_solution(12257813089730434626)
XLA Ops:
  0.6 88.1 %fused.1 = (f32[1,1]{1,0:T(1,128)}, bf16[4,64,1024]{2,1,0:T(8,128)(2,1)}, bf16[4,64,1024]{2,1,0:T(8,128)(2,1)}) custom-call(s32[8,64]{1,0:T(8,128)} %bitcast.2, bf16[4,64,1024]{2,1,0:T(8,128)(2,1)} %q_hbm.1, bf16[4,64,1024]{2,1,0:T(8,128)(2,1)} %p_hbm.1), custom_call_target="tpu_custom_call" | custom-call | tf_op jit(solution)/shard_map/fused/pallas_call | solution.py:661
  88.7 2.7 %finish.1 = (f32[1,1]{1,0:T(1,128)}, bf16[4,64,1024]{2,1,0:T(8,128)(2,1)}, bf16[4,64,1024]{2,1,0:T(8,128)(2,1)}) custom-call(f32[1,1]{1,0:T(1,128)} %get-tuple-element.9.loss_ref, bf16[4,64,1024]{2,1,0:T(8,128)(2,1)} %get-tuple-element.10.q_ref, bf16[4,64,1024]{2,1,0:T(8,128)(2,1)} %get-tuple-element.11.p_ref), custom_call_target="tpu_custom_call" | custom-call | tf_op jit(solution)/shard_map/finish/pallas_call | solution.py:671

commit v7 on v6

--- a/solution.py
+++ b/solution.py
@@ -354,10 +354,21 @@
                    for to, origin in zip(dp_peers, dp_from)]
     all_rows[me.inner] = rows_mine
     all_dense[me.dp] = dense_mine
-    for copy in stat_waits:
+    for copy in stat_waits[:len(in_peers)]:
         copy.wait_recv()
-    rows_all, dense_all = fold(all_rows[...]), fold(all_dense[...])
+    rows_all = fold(all_rows[...])
     row_lse[...] = rows_all
+    for b in range(per):
+        row = row_lse[b:b + 1] + 1.0
+        for i in range(cands):
+            probs = jnp.exp2(logit[b][i * rows:(i + 1) * rows] - row)
+            if i == 0:
+                hit = wide_lane == wide_sub + me.inner * rows
+                probs = probs - jnp.where(hit, 1.0, 0.0)
+            prod[b][2 * i:2 * i + 2, :, 0:queries] = probs.reshape(2, half, queries)
+    for copy in stat_waits[len(in_peers):]:
+        copy.wait_recv()
+    dense_all = fold(all_dense[...])
     pass_lse[...] = dense_all
     where = lax.broadcasted_iota(jnp.int32, rows_all.shape, 1) // rows
     loss_own = jnp.sum(jnp.where(where == me.inner, rows_all, 0.0))
@@ -365,17 +376,14 @@
     loss_mid[0] = loss_own - 2.0 * own_sum[...]
 
     def weigh(b):
-        row = row_lse[b:b + 1] + 1.0
         for i in range(cands):
             block = block_of(b, i)
             values = pass_lse[pl.ds(lax.rem(block, 32), 1)]
             pick = lane == sub + (block // 32) * 64
             col = jnp.sum(jnp.where(pick, values, 0.0), axis=1, keepdims=True) + 1.0
             z = logit[b][i * rows:(i + 1) * rows]
-            probs = jnp.exp2(z - row) + jnp.exp2(z - col)
-            if i == 0:
-                hit = wide_lane == wide_sub + me.inner * rows
-                probs = probs - jnp.where(hit, 1.0, 0.0)
+            probs = prod[b][2 * i:2 * i + 2, :, 0:queries].reshape(rows, queries)
+            probs = probs + jnp.exp2(z - col)
             weight[b][i * rows:(i + 1) * rows] = probs.astype(b16)
 
     def multiply(b):

time: 92 us -> 92 us (level)
  no operation moved by 1% of the time
where the time goes in v7:
time: 92 us; the launch traced here: 91.2 us
  Pallas kernels  90.4 us (98%)
    pallas_call x1, Pallas kernels, body(): pl.pallas_call(functools.partial(fused_kernel, (chunks, groups, inners),...  87.7 us
    pallas_call x1, Pallas kernels, body(): pl.pallas_call(finish_kernel, out_shape=(sds((1, 1), f32), sds(shape, b16...  2.74 us

profile of v7, /device:TPU:0, one launch (start us, length us, event | category | flops | bytes accessed | tf_op | source)
XLA Modules:
  0.0 91.2 jit_solution(17933151388521466931)
XLA Ops:
  0.6 87.7 %fused.1 = (f32[1,1]{1,0:T(1,128)}, bf16[4,64,1024]{2,1,0:T(8,128)(2,1)}, bf16[4,64,1024]{2,1,0:T(8,128)(2,1)}) custom-call(s32[8,64]{1,0:T(8,128)} %bitcast.2, bf16[4,64,1024]{2,1,0:T(8,128)(2,1)} %q_hbm.1, bf16[4,64,1024]{2,1,0:T(8,128)(2,1)} %p_hbm.1), custom_call_target="tpu_custom_call" | custom-call | tf_op jit(solution)/shard_map/fused/pallas_call | solution.py:669
  88.3 2.7 %finish.1 = (f32[1,1]{1,0:T(1,128)}, bf16[4,64,1024]{2,1,0:T(8,128)(2,1)}, bf16[4,64,1024]{2,1,0:T(8,128)(2,1)}) custom-call(f32[1,1]{1,0:T(1,128)} %get-tuple-element.9.loss_ref, bf16[4,64,1024]{2,1,0:T(8,128)(2,1)} %get-tuple-element.10.q_ref, bf16[4,64,1024]{2,1,0:T(8,128)(2,1)} %get-tuple-element.11.p_ref), custom_call_target="tpu_custom_call" | custom-call | tf_op jit(solution)/shard_map/finish/pallas_call | solution.py:679
